TPU v7x, 32 devices: a whole 2x2x4 slice. The times are simulated.
32 devices in a mesh: groups: 1, frame: 32 (over z, y, x, core).
Axes of the slice: x: 2, y: 2, z: 4, core: 2. Of those that a mesh axis runs over, the one named last changes fastest.
Arguments:
- feature_map: bfloat16 [32, 64, 128, 128], P('frame', 'groups'), may hold values from -6 to 6
- pixel_row: int32 [32, 128], P('frame', 'groups'), may hold values from 6 to 56
- pixel_column: int32 [32, 128], P('frame', 'groups'), may hold values from 6 to 120
- query_frame: int32 [128], P('groups'), may hold values from 0 to 31
- visible: int32 [32, 128], P(None, 'groups'), may hold values 0 or 1
- window_start: int32 [1], P('groups'), may hold values from 0 to 4095
- match_weight: bfloat16 [98, 384], replicated, may hold values from -0.625 to 0.625
- layer_gains: float32 [2, 2, 384], replicated, may hold values from 0.5 to 1.5
- joint_weight: bfloat16 [2, 384, 1152], replicated
- output_weight: bfloat16 [2, 384, 384], replicated, may hold values from -0.3125 to 0.3125
- expand_weight: bfloat16 [2, 384, 1536], replicated, may hold values from -0.3125 to 0.3125
- reduce_weight: bfloat16 [2, 1536, 384], replicated, may hold values from -0.15625 to 0.15625
Outputs:
- handed: bfloat16 [32, 128, 384], P('frame', 'groups')
All inputs are finite; a program needn't handle non-finite values.
Results may differ from a plain program's by a relative error of at most 0.015.
Values may be sent and summed in bfloat16 or wider, within the bound.
No kernel may reach another device: no remote copies, remote signals or barrier semaphores. Data moves between devices by JAX's collectives and lax.ppermute only.
A program may use at most 128 MiB of HBM per device.

v0:
```python
import math

import jax
import jax.numpy as jnp
from jax import lax
from jax.sharding import PartitionSpec as P

HEADS = 8
PATCH = 7


EPSILON = 1e-05


def normalize(values, weights):
    average = jnp.mean(values, axis=-1, keepdims=True)
    centred = values - average
    variance = jnp.mean(centred * centred, axis=-1, keepdims=True)
    return centred * lax.rsqrt(variance + EPSILON) * weights


def coarsen(feature_map):
    frames, height, breadth, channels = feature_map.shape
    shaped = feature_map.astype(jnp.float32).reshape(
        frames, height // 2, 2, breadth // 2, 2, channels
    )
    return (jnp.sum(shaped, axis=(2, 4)) * 0.25).astype(jnp.bfloat16)


def time_embedding(absolute, features):
    half_way = features // 2
    frequency = jnp.exp(-math.log(10000.0) * jnp.arange(half_way, dtype=jnp.float32) / half_way)
    angles = absolute.astype(jnp.float32)[:, None] * frequency[None, :]
    return jnp.concatenate([jnp.sin(angles), jnp.cos(angles)], axis=-1)


def prepare(tokens, gain_pair, joint_weight):
    stream = tokens.astype(jnp.float32)
    hidden = normalize(stream, gain_pair[0]).astype(jnp.bfloat16)
    projected = jnp.einsum(
        "abd,de->abe", hidden, joint_weight, preferred_element_type=jnp.float32
    ).astype(jnp.bfloat16)
    return (stream, projected)


def finish(stream, attended, gain_pair, output_weight, expand_weight, reduce_weight):
    stream = stream + jnp.einsum(
        "abd,de->abe", attended, output_weight, preferred_element_type=jnp.float32
    )
    hidden = normalize(stream, gain_pair[1]).astype(jnp.bfloat16)
    widened = jax.nn.gelu(
        jnp.einsum("abd,de->abe", hidden, expand_weight, preferred_element_type=jnp.float32),
        approximate=True,
    ).astype(jnp.bfloat16)
    return (
        stream
        + jnp.einsum("abe,ed->abd", widened, reduce_weight, preferred_element_type=jnp.float32)
    ).astype(jnp.bfloat16)


def cross_block(
    tokens, allowed, gain_pair, joint_weight, output_weight, expand_weight, reduce_weight
):
    frames, points, features = tokens.shape
    per_head = features // HEADS
    stream, projected = prepare(tokens, gain_pair, joint_weight)
    queries = projected[..., :features]
    keyset = projected[..., features : 2 * features].reshape(frames, points, HEADS, per_head)
    values = projected[..., 2 * features :].reshape(frames, points, HEADS, per_head)
    block_rows = min(512, points)
    block_count = points // block_rows
    grouped = queries.reshape(frames, block_count, block_rows, HEADS, per_head)
    key_ids = jnp.arange(points)

    def attend(which):
        chosen = lax.dynamic_index_in_dim(grouped, which, 1, keepdims=False)
        scores = jnp.einsum(
            "gqhe,gkhe->ghqk", chosen, keyset, preferred_element_type=jnp.float32
        ) / math.sqrt(per_head)
        query_ids = which * block_rows + jnp.arange(block_rows)
        permitted = allowed[:, None, None, :] | (query_ids[:, None] == key_ids[None, :])[None, None]
        scores = jnp.where(permitted, scores, -1e30)
        attn_weights = jax.nn.softmax(scores, axis=-1).astype(jnp.bfloat16)
        return jnp.einsum(
            "ghqk,gkhe->gqhe", attn_weights, values, preferred_element_type=jnp.float32
        ).astype(jnp.bfloat16)

    pieces = lax.map(attend, jnp.arange(block_count))
    attended = jnp.transpose(pieces, (1, 0, 2, 3, 4)).reshape(frames, points, features)
    return finish(stream, attended, gain_pair, output_weight, expand_weight, reduce_weight)


def time_block(
    tokens, allowed, gain_pair, joint_weight, output_weight, expand_weight, reduce_weight
):
    length, groups, features = tokens.shape
    per_head = features // HEADS
    stream, projected = prepare(tokens, gain_pair, joint_weight)
    queries = projected[..., :features].reshape(length, groups, HEADS, per_head)
    keyset = projected[..., features : 2 * features].reshape(length, groups, HEADS, per_head)
    values = projected[..., 2 * features :].reshape(length, groups, HEADS, per_head)
    scores = jnp.einsum(
        "qghe,kghe->ghqk", queries, keyset, preferred_element_type=jnp.float32
    ) / math.sqrt(per_head)
    diagonal = jnp.arange(length)[:, None] == jnp.arange(length)[None, :]
    permitted = jnp.transpose(allowed)[:, None, None, :] | diagonal[None, None]
    scores = jnp.where(permitted, scores, -1e30)
    attn_weights = jax.nn.softmax(scores, axis=-1).astype(jnp.bfloat16)
    attended = jnp.einsum(
        "ghqk,kghe->qghe", attn_weights, values, preferred_element_type=jnp.float32
    ).astype(jnp.bfloat16)
    attended = attended.reshape(length, groups, features)
    return finish(stream, attended, gain_pair, output_weight, expand_weight, reduce_weight)


def shards(
    feature_map,
    pixel_row,
    pixel_column,
    query_frame,
    visible,
    window_start,
    match_weight,
    layer_gains,
    joint_weight,
    output_weight,
    expand_weight,
    reduce_weight,
):
    frames, height, breadth, channels = feature_map.shape
    points = query_frame.shape[0]
    features = match_weight.shape[1]
    devices = lax.axis_size("frame")
    position = lax.axis_index("frame")
    first_frame = position * frames
    pooled = coarsen(feature_map)
    frame_ids = first_frame + jnp.arange(frames, dtype=jnp.int32)
    owned = query_frame[None, :] == frame_ids[:, None]
    flat_fine = feature_map.reshape(frames, height * breadth, channels)
    flat_coarse = pooled.reshape(frames, height // 2 * (breadth // 2), channels)
    fine_index = pixel_row * breadth + pixel_column
    coarse_index = pixel_row // 2 * (breadth // 2) + pixel_column // 2

    def take_rows(flat_map, cell_index):
        return jax.vmap(lambda one_map, one_index: one_map[one_index])(flat_map, cell_index)

    def anchor_rows(flat_map, cell_index):
        picked = take_rows(flat_map, cell_index).astype(jnp.float32)
        return jnp.sum(jnp.where(owned[:, :, None], picked, 0.0), axis=0)

    fine_term = anchor_rows(flat_fine, fine_index)
    coarse_term = anchor_rows(flat_coarse, coarse_index)
    fine_feat, coarse_feat = lax.psum((fine_term, coarse_term), "frame")
    cells = jnp.arange(PATCH * PATCH, dtype=jnp.int32)
    row_offset = cells // PATCH - 3
    column_offset = cells % PATCH - 3

    def correlate(flat_map, row_at, column_at, stride_cells, anchor):
        cell_index = (row_at[:, :, None] + row_offset) * stride_cells + (
            column_at[:, :, None] + column_offset
        )
        patches = take_rows(flat_map, cell_index.reshape(frames, -1)).reshape(
            frames, points, PATCH * PATCH, channels
        )
        return jnp.einsum(
            "fpjc,pc->fpj", patches, anchor.astype(jnp.bfloat16), preferred_element_type=jnp.float32
        ) / math.sqrt(channels)

    fine_part = correlate(flat_fine, pixel_row, pixel_column, breadth, fine_feat)
    coarse_part = correlate(
        flat_coarse, pixel_row // 2, pixel_column // 2, breadth // 2, coarse_feat
    )
    matches = jnp.concatenate([fine_part, coarse_part], axis=-1).astype(jnp.bfloat16)
    embedding = time_embedding(window_start[0] + frame_ids, features)
    projected = jnp.einsum("fpj,jd->fpd", matches, match_weight, preferred_element_type=jnp.float32)
    tokens = (projected + embedding[:, None, :]).astype(jnp.bfloat16)
    allowed_here = lax.dynamic_slice_in_dim(visible, first_frame, frames, 0) == 1
    crossed = cross_block(
        tokens,
        allowed_here,
        layer_gains[0],
        joint_weight[0],
        output_weight[0],
        expand_weight[0],
        reduce_weight[0],
    )
    by_track = lax.all_to_all(crossed, "frame", split_axis=1, concat_axis=0, tiled=True)
    per_device = points // devices
    allowed_track = lax.dynamic_slice_in_dim(visible, position * per_device, per_device, 1) == 1
    tracked = time_block(
        by_track,
        allowed_track,
        layer_gains[1],
        joint_weight[1],
        output_weight[1],
        expand_weight[1],
        reduce_weight[1],
    )
    half_way = tracked.shape[0] // 2
    final_rows = jnp.broadcast_to(tracked[-1:], (tracked.shape[0] - half_way,) + tracked.shape[1:])
    source_tokens = jnp.concatenate([tracked[half_way:], final_rows], axis=0)
    handed = lax.all_to_all(source_tokens, "frame", split_axis=0, concat_axis=1, tiled=True)
    return handed


def solution(mesh):
    placed = (
        P("frame", "groups", None, None),
        P("frame", "groups"),
        P("frame", "groups"),
        P("groups"),
        P(None, "groups"),
        P("groups"),
        P(),
        P(),
        P(),
        P(),
        P(),
        P(),
    )
    return jax.shard_map(
        shards, mesh=mesh, in_specs=placed, out_specs=P("frame", "groups", None), check_vma=False
    )
```

profile of v0, /device:TPU:0, one launch (start us, length us, event | category | flops | bytes accessed | tf_op | source)
XLA Modules:
  0.0 184.0 jit_solution(16434008931723907015)
XLA Ops:
  0.7 0.7 broadcast_compare_fusion
  1.4 0.7 fusion.123
  2.1 0.8 slice_reduce_fusion
  2.9 0.7 compare_bitcast_fusion
  3.8 0.2 add.378
  4.1 0.2 add.369
  4.4 0.2 add.381
  4.6 0.2 add.363
  4.8 0.7 add.365
  5.6 0.2 add.366
  5.8 0.7 add.360
  6.5 0.2 add.361
  6.8 0.1 compare_select_fusion.1
  6.9 0.1 fusion.117
  7.1 0.1 fusion.118
  7.2 5.2 %convert_reduce_fusion = f32[32,64,128]{2,1,0:T(8,128)S(1)} fusion(bf16[32,2,64,2,128]{4,3,2,1,0:T(2,128)(2,1)} %bitcast.151), kind=kLoop, calls=%fused_computation.6 | loop fusion | flops 1835008 | bytes 3145728 | tf_op jit(solution)/shard_map/reduce_sum | solution.py:27
  12.5 0.1 multiply_convert_fusion
  12.6 1.0 gather_fusion
  13.6 1.0 gather_fusion.2
  14.6 38.5 %gather_fusion.3 = bf16[6272,128]{1,0:T(8,128)(2,1)} fusion(bf16[1,2048,128]{2,1,0:T(8,128)(2,1)S(1)} %bitcast.150, s32[6272]{0:T(1024)S(1)} %fusion.118), kind=kCustom, calls=%fused_computation.3 | custom fusion | bytes 3261440 | tf_op jit(solution)/shard_map/vmap()/gather | solution.py:145
  53.2 3.7 %reshape.653 = bf16[128,49,128]{2,1,0:T(8,128)(2,1)} reshape(bf16[6272,128]{1,0:T(8,128)(2,1)} %gather_fusion.3) | data formatting | bytes 3211264 | tf_op jit(solution)/shard_map/reshape.30
  56.9 43.0 %all-reduce.2 = (bf16[128,128]{1,0:T(8,128)(2,1)S(1)}, bf16[128,128]{1,0:T(8,128)(2,1)S(1)}) all-reduce(f32[128,128]{1,0:T(8,128)S(1)} %get-tuple-element.47, f32[128,128]{1,0:T(8,128)S(1)} %get-tuple-element.46), channel_id=1, replica_groups=mesh['groups'=1,'frame'=32] {'frame'}, use_global_device_ids=true, to_apply=%region_2.3 | all-reduce | flops 32768 | bytes 196608 | tf_op jit(solution)/shard_map/psum | solution.py:153
  99.9 2.5 %fusion.103 = f32[128,1,49]{2,1,0:T(1,128)S(1)} fusion(bf16[128,49,128]{2,1,0:T(8,128)(2,1)} %reshape.653, bf16[128,128,1]{1,0,2:T(8,128)(2,1)S(1)} %bitcast.169), kind=kOutput, calls=%fused_computation.108 | convolution fusion | flops 1605632 | bytes 1663488 | tf_op jit(solution)/shard_map/fpjc,pc->fpj/dot_general | solution.py:165
  102.5 38.6 %gather_fusion.1 = bf16[6272,128]{1,0:T(8,128)(2,1)} fusion(bf16[1,8192,128]{2,1,0:T(8,128)(2,1)S(1)} %bitcast.153, s32[6272]{0:T(1024)S(1)} %fusion.117), kind=kCustom, calls=%fused_computation.1 | custom fusion | bytes 3261440 | tf_op jit(solution)/shard_map/vmap()/gather | solution.py:145
  141.0 2.5 %reshape.650 = bf16[128,49,128]{2,1,0:T(8,128)(2,1)S(1)} reshape(bf16[6272,128]{1,0:T(8,128)(2,1)} %gather_fusion.1) | data formatting | bytes 3211264 | tf_op jit(solution)/shard_map/reshape.7
  143.6 1.1 fusion.105
  144.6 0.1 maximum_reduce_fusion
  144.7 0.3 fusion.141
  145.1 0.2 multiply_reduce_fusion.3
  145.3 0.4 fusion.2
  145.7 0.1 copy.52
  145.8 0.1 copy.51
  146.0 0.4 fusion.142
  146.3 0.3 fusion.7
  146.6 0.1 copy.50
  146.8 0.3 convolution_convert_fusion.3
  147.1 0.3 fusion.143
  147.4 0.2 multiply_reduce_fusion.2
  147.6 2.4 %fusion.36 = bf16[1,128,384]{2,1,0:T(8,128)(2,1)S(1)} fusion(f32[128,384]{1,0:T(8,128)S(1)} %get-tuple-element.51, bf16[2,1536,384]{2,1,0:T(8,128)(2,1)} %param.23, bf16[2,384,1536]{2,1,0:T(8,128)(2,1)} %param.22, f32[384]{0:T(512)S(1)} %get-tuple-element.20, f32[128]{0:T(128)S(1)} %add_rsqrt_fusion.2, f32[128]{0:T(128)S(1)} %broadcast_multiply_fusion.2), kind=kOutput, calls=%fused_computation.44 | convolution fusion | flops 304054272 | bytes 2853888 | tf_op jit(solution)/shard_map/abe,ed->abd/dot_general | solution.py:57
  150.0 0.2 copy.89
  150.2 0.5 broadcast.545
  150.7 1.2 reduce.33
  151.9 0.7 reshape.722
  152.6 4.4 %all-to-all-start = ((bf16[32,2,768]{2,1,0:T(2,128)(2,1)}), bf16[32,2,768]{2,1,0:T(2,128)(2,1)S(1)}, u32[]{:S(2)}, u32[]{:S(2)}) async-start(bf16[32,2,768]{2,1,0:T(2,128)(2,1)} %reshape.722), calls=%async_computation | async-start | bytes 196608 | tf_op jit(solution)/shard_map/all_to_all | solution.py:187
  157.2 0.1 copy.56
  157.3 0.1 broadcast_or_fusion
  157.4 7.5 %all-to-all-done = bf16[32,2,768]{2,1,0:T(2,128)(2,1)S(1)} async-done(((bf16[32,2,768]{2,1,0:T(2,128)(2,1)}), bf16[32,2,768]{2,1,0:T(2,128)(2,1)S(1)}, u32[]{:S(2)}, u32[]{:S(2)}) %all-to-all-start) | async-done | bytes 98336 | tf_op jit(solution)/shard_map/all_to_all | solution.py:187
  164.9 1.0 convert_reduce_fusion.2
  166.0 1.9 %multiply_reduce_fusion.1 = f32[128]{0:T(128)S(1)} fusion(f32[128]{0:T(128)S(1)} %broadcast_multiply_fusion.1, bf16[128,1,384]{2,1,0:T(2,128)(2,1)S(1)} %reshape.723), kind=kLoop, calls=%fused_computation.90 | loop fusion | flops 196480 | bytes 99328 | tf_op jit(solution)/shard_map/reduce_sum | solution.py:18
  167.9 0.7 convert_reduce_fusion.3
  168.7 0.3 convolution_convert_fusion
  169.0 0.2 reshape.659
  169.3 0.2 reshape.660
  169.5 0.3 fusion.8
  169.8 0.2 fusion.144
  170.0 0.2 reshape.658
  170.2 0.3 fusion.21
  170.5 0.1 copy.61
  170.6 0.2 reshape.661
  170.8 0.3 fusion.145
  171.1 0.2 multiply_reduce_fusion
  171.3 2.4 %fusion.30 = bf16[32,4,384]{2,0,1:T(8,128)(2,1)S(1)} fusion(f32[32,4,384]{2,0,1:T(8,128)S(1)} %get-tuple-element.53, bf16[2,1536,384]{2,1,0:T(8,128)(2,1)} %param.23, bf16[2,384,1536]{2,1,0:T(8,128)(2,1)} %param.22, f32[384]{0:T(512)S(1)} %get-tuple-element.19, f32[32,4]{0,1:T(4,128)S(1)} %add_rsqrt_fusion, f32[32,4]{0,1:T(4,128)S(1)} %broadcast_multiply_fusion), kind=kOutput, calls=%fused_computation.41 | convolution fusion | flops 304054272 | bytes 2856960 | tf_op jit(solution)/shard_map/abe,ed->abd/dot_general | solution.py:57
  173.9 9.5 %all_to_all.21 = bf16[32,4,384]{2,1,0:T(4,128)(2,1)S(1)} all-to-all(bf16[32,4,384]{2,1,0:T(4,128)(2,1)S(1)} %copy.63), channel_id=1, replica_groups=mesh['groups'=1,'frame'=32] {'frame'}, dimensions={0} | all-to-all | bytes 196608 | tf_op jit(solution)/shard_map/all_to_all | solution.py:202
  183.3 0.7 all_to_all.8
  (48 shorter events, 1.0 us)
Async XLA Ops:
  0.0 144.7 %copy-start = (bf16[98,384]{1,0:T(8,128)(2,1)S(1)}, bf16[98,384]{1,0:T(8,128)(2,1)}, u32[]{:S(2)}) copy-start(bf16[98,384]{1,0:T(8,128)(2,1)} %param.18) | copy-start | bytes 225796
  7.2 5.4 %copy-start.1 = (bf16[1,64,128,128]{3,2,1,0:T(8,128)(2,1)S(1)}, bf16[1,64,128,128]{3,2,1,0:T(8,128)(2,1)}, u32[]{:S(2)}) copy-start(bf16[1,64,128,128]{3,2,1,0:T(8,128)(2,1)} %param.12) | copy-start | bytes 6291460
  143.6 1.7 copy-start.3
  145.7 1.3 copy-start.2
  147.6 9.5 %copy-start.5 = (s32[32,128]{1,0:T(8,128)S(1)}, s32[32,128]{1,0:T(8,128)}, u32[]{:S(2)}) copy-start(s32[32,128]{1,0:T(8,128)} %param.16) | copy-start | bytes 49156
  150.0 18.6 %copy-start.4 = (bf16[2,384,1152]{2,1,0:T(8,128)(2,1)S(1)}, bf16[2,384,1152]{2,1,0:T(8,128)(2,1)}, u32[]{:S(2)}) copy-start(bf16[2,384,1152]{2,1,0:T(8,128)(2,1)} %param.20) | copy-start | bytes 5308420
  152.6 12.2 %all-to-all-start = ((bf16[32,2,768]{2,1,0:T(2,128)(2,1)}), bf16[32,2,768]{2,1,0:T(2,128)(2,1)S(1)}, u32[]{:S(2)}, u32[]{:S(2)}) async-start(bf16[32,2,768]{2,1,0:T(2,128)(2,1)} %reshape.722), calls=%async_computation | async-start | bytes 196608 | tf_op jit(solution)/shard_map/all_to_all | solution.py:187
where the time goes:
time: 185 us; the launch traced here: 184 us
  local copies, waits for them, and re-layouts  92.9 us (50%)
  blocking collectives  52.5 us (28%)
  other arithmetic  13.9 us (8%)
  matrix products  11.6 us (6%)
  waiting for transfers between devices  7.49 us (4%)
  starting transfers between devices  4.41 us (2%)
    gather x8, local copies, waits for them, and re-layouts, take_rows(): one_map[one_index]  79.1 us
    psum x1, blocking collectives, shards(): fine_feat, coarse_feat = lax.psum((fine_term, coarse_term), 'frame')  43 us
    all_to_all x1, blocking collectives, shards(): lax.all_to_all(source_tokens, 'frame', split_axis=0, concat_axis=1, tiled...  9.48 us
    all_to_all x1, waiting for transfers between devices, shards(): lax.all_to_all(crossed, 'frame', split_axis=1, concat_axis=0, tiled=True)  7.49 us
    another operation x2, local copies, waits for them, and re-layouts  6.19 us
    reduce_sum x1, other arithmetic, coarsen(): return (jnp.sum(shaped, axis=(2, 4)) * 0.25).astype(jnp.bfloat16)  5.23 us
    dot_general x2, matrix products, finish(): jnp.einsum('abe,ed->abd', widened, reduce_weight, preferred_element_type=...  4.76 us
    all_to_all x1, starting transfers between devices, shards(): lax.all_to_all(crossed, 'frame', split_axis=1, concat_axis=0, tiled=True)  4.41 us
  transfers between devices with their start and end apart: 1, of which 1 were waited for; matrix products, arithmetic and copies ran while one was open for 0% of the time, Pallas kernels for 0%

commit v1 on v0

v1 whole, which is shorter than its diff:
```python
import math

import jax
import jax.numpy as jnp
from jax import lax
from jax.experimental import pallas as pl
from jax.experimental.pallas import tpu as pltpu
from jax.sharding import PartitionSpec as P

HEADS = 8
PATCH = 7
EPSILON = 1e-05
LANES = 128
TILE = 16
F32 = jnp.float32
BF16 = jnp.bfloat16
VMEM = pltpu.MemorySpace.VMEM
SMEM = pltpu.MemorySpace.SMEM


def normalize(values, weights):
    average = jnp.mean(values, axis=-1, keepdims=True)
    centred = values - average
    variance = jnp.mean(centred * centred, axis=-1, keepdims=True)
    return centred * lax.rsqrt(variance + EPSILON) * weights


def time_embedding(absolute, features):
    half_way = features // 2
    frequency = jnp.exp(-math.log(10000.0) * jnp.arange(half_way, dtype=F32) / half_way)
    angles = absolute.astype(F32)[:, None] * frequency[None, :]
    return jnp.concatenate([jnp.sin(angles), jnp.cos(angles)], axis=-1)


def iota(shape, axis):
    return lax.broadcasted_iota(jnp.int32, shape, axis)


def matmul(left, right):
    return jnp.dot(left, right, preferred_element_type=F32)


def matmul_nt(left, right):
    return lax.dot_general(left, right, (((1,), (1,)), ((), ())), preferred_element_type=F32)


def pack_kernel(slots, round_ref, query_ref, row_ref, column_ref, map_ref, out_ref, tiles, where_ref, fine, coarse, sems):
    me = lax.axis_index("frame")
    points = query_ref.shape[1]
    base = round_ref[0] * slots

    def tile_copy(slot, row, column):
        return pltpu.make_async_copy(
            map_ref.at[0, pl.ds(row // 2 * 2, 2), pl.ds(pl.multiple_of(column // TILE * TILE, TILE), TILE), :],
            tiles.at[slot],
            sems.at[slot],
        )

    def scan(point, found):
        mine = query_ref[0, point] == me
        slot = found - base

        @pl.when(mine & (slot >= 0) & (slot < slots))
        def _():
            row = row_ref[0, point]
            column = column_ref[0, point]
            tile_copy(slot, row, column).start()
            where_ref[slot] = row % 2 * TILE + column % TILE

        return found + mine.astype(jnp.int32)

    found = lax.fori_loop(0, points, scan, jnp.int32(0), unroll=8)
    count = jnp.clip(found - base, 0, slots)
    fine[...] = jnp.zeros_like(fine)
    coarse[...] = jnp.zeros_like(coarse)
    cell = iota((2, TILE, LANES), 0) * TILE + iota((2, TILE, LANES), 1)

    def select(slot, carry):
        tile_copy(slot, 0, 0).wait()
        at = where_ref[slot]
        tile = tiles[slot].astype(F32)
        fine[pl.ds(slot, 1), :] = jnp.sum(jnp.where(cell == at, tile, 0.0), axis=(0, 1))[None]
        near = cell % TILE // 2 == at % TILE // 2
        coarse[pl.ds(slot, 1), :] = jnp.sum(jnp.where(near, tile, 0.0), axis=(0, 1))[None] * 0.25
        return carry

    lax.fori_loop(0, count, select, 0)
    block = jnp.concatenate([fine[...], coarse[...]], axis=1).astype(BF16)
    out_ref[...] = jnp.broadcast_to(block[None], out_ref.shape)


def ranks(query_row):
    points = query_row.shape[1]
    across = jnp.broadcast_to(query_row.astype(F32), (points, points))
    down = across.T
    earlier = (across == down) & (iota((points, points), 1) < iota((points, points), 0))
    rank = jnp.sum(jnp.where(earlier, 1.0, 0.0), axis=1, keepdims=True)
    return down[:, :1].astype(jnp.int32), rank.astype(jnp.int32)


def unpack(query_row, received, slots, base):
    frame, rank = ranks(query_row)
    points, total = frame.shape[0], received.shape[0]
    inside = (rank >= base) & (rank < base + slots)
    at = jnp.where(inside, frame * slots + rank - base, -1)
    chosen = jnp.where(iota((points, total), 1) == at, 1.0, 0.0).astype(BF16)
    return matmul(chosen, received)


def attention(queries, keyset, values, permitted):
    rows, features = queries.shape
    per_head = features // HEADS
    head_of = iota((1, features), 1) // per_head
    spread = jnp.concatenate(
        [jnp.where(head_of == head, queries, 0) for head in range(HEADS)], axis=0
    )
    scores = matmul_nt(spread, keyset) * (1.0 / math.sqrt(per_head))
    outcome = None
    parts = []
    for head in range(HEADS):
        part = jnp.where(permitted, scores[head * rows : (head + 1) * rows], -1e30)
        part = jnp.exp(part - jnp.max(part, axis=-1, keepdims=True))
        parts.append((part / jnp.sum(part, axis=-1, keepdims=True)).astype(BF16))
    mixed = matmul(jnp.concatenate(parts, axis=0), values)
    for head in range(HEADS):
        term = jnp.where(head_of == head, mixed[head * rows : (head + 1) * rows], 0.0)
        outcome = term if outcome is None else outcome + term
    return outcome.astype(BF16)


def finish(stream, attended, gain, output_weight, expand_weight, reduce_weight):
    stream = stream + matmul(attended, output_weight)
    hidden = normalize(stream, gain).astype(BF16)
    widened = jax.nn.gelu(matmul(hidden, expand_weight), approximate=True).astype(BF16)
    return stream + matmul(widened, reduce_weight)


def frame_kernel(
    slots,
    row_ref,
    column_ref,
    query_ref,
    received_ref,
    extra_ref,
    map_ref,
    visible_ref,
    embedding_ref,
    match_ref,
    gains_ref,
    joint_ref,
    output_ref,
    expand_ref,
    reduce_ref,
    out_ref,
    corr,
    fine,
    coarse,
    staged,
):
    me = lax.axis_index("frame")
    points = query_ref.shape[1]
    _, height, breadth, channels = map_ref.shape
    features = match_ref.shape[1]
    devices = out_ref.shape[0]
    received = received_ref[...].reshape(devices * slots, 2 * channels)
    anchors = (unpack(query_ref[...], received, slots, 0) + extra_ref[...].astype(F32)).astype(BF16)
    lane = iota((1, LANES), 1)
    feats = []
    for start in range(0, points, LANES):
        both = jnp.concatenate(
            [anchors[start : start + LANES, :channels], anchors[start : start + LANES, channels:]], axis=0
        )

        def correlate(pair, carry):
            cells = map_ref[0, pl.ds(pair * 2, 2)].reshape(2 * breadth, channels)
            product = matmul_nt(both, cells)
            at = pl.multiple_of(pair * 4 * LANES, 4 * LANES)
            corr[pl.ds(at, 2 * LANES), :] = product[:, :breadth]
            corr[pl.ds(at + 2 * LANES, 2 * LANES), :] = product[:, breadth:]
            return carry

        lax.fori_loop(0, height // 2, correlate, 0, unroll=2)

        def extract(point, carry):
            row = row_ref[0, start + point]
            column = column_ref[0, start + point]
            window = corr[pl.ds((row - 3) * 2 * LANES + point, 8, stride=2 * LANES), :]
            fine[pl.ds(pl.multiple_of(point * 8, 8), 8), :] = pltpu.roll(window, LANES + 3 - column, 1)
            top = row // 2 * 2 - 6
            at = top * 2 * LANES + LANES + point
            pairs = (
                corr[pl.ds(at, 8, stride=4 * LANES), :]
                + corr[pl.ds(at + 2 * LANES, 8, stride=4 * LANES), :]
            )
            coarse[pl.ds(pl.multiple_of(point * 8, 8), 8), :] = pltpu.roll(
                pairs, LANES + 6 - column // 2 * 2, 1
            )
            return carry

        lax.fori_loop(0, LANES, extract, 0, unroll=8)

        def merged(ref):
            result = None
            for k in range(PATCH):
                part = ref[pl.ds(k, LANES, stride=8), :]
                result = part if k == 0 else jnp.where(lane // TILE == k, pltpu.roll(part, k * TILE, 1), result)
            return result

        scale = 1.0 / math.sqrt(channels)
        level_0 = merged(fine) * scale
        level_1 = merged(coarse)
        level_1 = (level_1 + pltpu.roll(level_1, LANES - 1, 1)) * (0.25 * scale)
        feats.append(jnp.concatenate([level_0, level_1], axis=1).astype(BF16))
    matches = jnp.concatenate(feats, axis=0)
    cells = match_ref.shape[0]
    place = iota((2 * LANES, cells), 0)
    level = place // LANES
    k, m = place % LANES // TILE, place % TILE
    m_at = jnp.where(level == 0, m, m // 2)
    valid = (k < PATCH) & (m_at < PATCH) & ((level == 0) | (m % 2 == 0))
    wanted = jnp.where(valid, level * PATCH * PATCH + k * PATCH + m_at, -1)
    pick = jnp.where(iota((2 * LANES, cells), 1) == wanted, 1.0, 0.0).astype(BF16)
    weights = matmul(pick, match_ref[...]).astype(BF16)
    tokens = (matmul(matches, weights) + embedding_ref[...]).astype(BF16)

    stream = tokens.astype(F32)
    hidden = normalize(stream, gains_ref[0, 0:1, :]).astype(BF16)
    projected = matmul(hidden, joint_ref[0]).astype(BF16)
    allowed = visible_ref[pl.ds(me, 1), :] == 1
    permitted = allowed | (iota((points, points), 0) == iota((points, points), 1))
    attended = attention(
        projected[:, :features], projected[:, features : 2 * features], projected[:, 2 * features :], permitted
    )
    crossed = finish(stream, attended, gains_ref[0, 1:2, :], output_ref[0], expand_ref[0], reduce_ref[0])
    pad_rows = out_ref.shape[1]
    chunks = features // LANES
    for i in range(points // devices):
        for c in range(chunks):
            staged[pl.ds(i * chunks + c, devices, stride=pad_rows), :] = crossed[
                i * devices : (i + 1) * devices, c * LANES : (c + 1) * LANES
            ]
    out_ref[...] = staged[...].astype(BF16).reshape(out_ref.shape)


def track_kernel(
    per_device,
    received_ref,
    visible_ref,
    gains_ref,
    joint_ref,
    output_ref,
    expand_ref,
    reduce_ref,
    out_ref,
    staged,
):
    me = lax.axis_index("frame")
    length, pad_rows, _ = received_ref.shape
    features = output_ref.shape[1]
    chunks = features // LANES
    points = visible_ref.shape[1]
    devices = out_ref.shape[0]
    half_way = length // 2
    staged[...] = received_ref[...].reshape(length * pad_rows, LANES).astype(F32)
    stream = jnp.concatenate(
        [
            jnp.concatenate(
                [staged[pl.ds(i * chunks + c, length, stride=pad_rows), :] for c in range(chunks)], axis=1
            )
            for i in range(per_device)
        ],
        axis=0,
    )
    total = per_device * length
    hidden = normalize(stream, gains_ref[1, 0:1, :]).astype(BF16)
    projected = matmul(hidden, joint_ref[1]).astype(BF16)

    def later(array):
        return jnp.concatenate(
            [array[i * length + half_way : (i + 1) * length] for i in range(per_device)], axis=0
        )

    rest = length - half_way
    lane = iota((points, total), 1)
    pick = jnp.where(iota((points, total), 0) == lane // length * devices + me, 1.0, 0.0).astype(BF16)
    seen = matmul(jnp.where(visible_ref[...] == 1, 1.0, 0.0).astype(BF16), pick)
    seen = jnp.where(iota((length, total), 1) % length == iota((length, total), 0), seen, 0.0)
    allowed = jnp.sum(seen, axis=0, keepdims=True) > 0.5
    query_at = iota((per_device * rest, total), 0)
    key_at = iota((per_device * rest, total), 1)
    same_point = query_at // rest == key_at // length
    same_frame = query_at % rest + half_way == key_at % length
    permitted = same_point & (allowed | same_frame)
    attended = attention(
        later(projected[:, :features]),
        projected[:, features : 2 * features],
        projected[:, 2 * features :],
        permitted,
    )
    tracked = finish(later(stream), attended, gains_ref[1, 1:2, :], output_ref[1], expand_ref[1], reduce_ref[1])
    for i in range(per_device):
        for c in range(chunks):
            piece = tracked[i * rest : (i + 1) * rest, c * LANES : (c + 1) * LANES]
            at = i * chunks + c
            staged[pl.ds(at, rest, stride=pad_rows), :] = piece
            staged[pl.ds(rest * pad_rows + at, half_way, stride=pad_rows), :] = jnp.broadcast_to(
                piece[rest - 1 :], (half_way, LANES)
            )
    out_ref[...] = staged[...].astype(BF16).reshape(out_ref.shape)


def layout_kernel(received_ref, out_ref, staged):
    devices, pad_rows, _ = received_ref.shape
    _, points, features = out_ref.shape
    chunks = features // LANES
    staged[...] = received_ref[...].reshape(devices * pad_rows, LANES).astype(F32)
    for i in range(points // devices):
        for c in range(chunks):
            out_ref[0, i * devices : (i + 1) * devices, c * LANES : (c + 1) * LANES] = staged[
                pl.ds(i * chunks + c, devices, stride=pad_rows), :
            ].astype(BF16)


def shards(
    feature_map,
    pixel_row,
    pixel_column,
    query_frame,
    visible,
    window_start,
    match_weight,
    layer_gains,
    joint_weight,
    output_weight,
    expand_weight,
    reduce_weight,
):
    frames, height, breadth, channels = feature_map.shape
    points = query_frame.shape[0]
    features = match_weight.shape[1]
    devices = lax.axis_size("frame")
    position = lax.axis_index("frame")
    per_device = points // devices
    slots = TILE * -(-4 * per_device // TILE)
    pad_rows = TILE * -(-per_device * (features // LANES) // TILE)
    query_row = query_frame.reshape(1, points)
    vmem = pl.BlockSpec(memory_space=VMEM)
    smem = pl.BlockSpec(memory_space=SMEM)

    pack = pl.pallas_call(
        lambda *refs: pack_kernel(slots, *refs),
        out_shape=jax.ShapeDtypeStruct((devices, slots, 2 * channels), BF16),
        in_specs=[smem, smem, smem, smem, pl.BlockSpec(memory_space=pl.ANY)],
        out_specs=vmem,
        scratch_shapes=[
            pltpu.VMEM((slots, 2, TILE, LANES), BF16),
            pltpu.SMEM((slots,), jnp.int32),
            pltpu.VMEM((slots, LANES), F32),
            pltpu.VMEM((slots, LANES), F32),
            pltpu.SemaphoreType.DMA((slots,)),
        ],
        name="pack",
    )

    def exchange(block):
        return lax.all_to_all(block, "frame", split_axis=0, concat_axis=0, tiled=True)

    def send_round(which):
        return exchange(pack(which.reshape(1), query_row, pixel_row, pixel_column, feature_map))

    received = send_round(jnp.int32(0))
    load = jnp.sum(query_frame[:, None] == jnp.arange(devices)[None, :], axis=0)
    rounds = lax.pmax((jnp.max(load) + slots - 1) // slots, "groups")

    def next_round(state):
        which, extra = state
        again = send_round(which).reshape(devices * slots, 2 * channels)
        return which + 1, extra + unpack(query_row, again, slots, which * slots).astype(BF16)

    _, extra = lax.while_loop(
        lambda state: state[0] < rounds, next_round, (jnp.int32(1), jnp.zeros((points, 2 * channels), BF16))
    )
    frame_ids = position * frames + jnp.arange(frames, dtype=jnp.int32)
    embedding = time_embedding(window_start[0] + frame_ids, features)
    crossed = pl.pallas_call(
        lambda *refs: frame_kernel(slots, *refs),
        out_shape=jax.ShapeDtypeStruct((devices, pad_rows, LANES), BF16),
        in_specs=[smem, smem] + [vmem] * 12,
        out_specs=vmem,
        scratch_shapes=[
            pltpu.VMEM(((height + 2) * 2 * LANES, LANES), F32),
            pltpu.VMEM((8 * LANES, LANES), F32),
            pltpu.VMEM((8 * LANES, LANES), F32),
            pltpu.VMEM((devices * pad_rows, LANES), F32),
        ],
        name="frame_block",
    )(
        pixel_row,
        pixel_column,
        query_row,
        received,
        extra,
        feature_map,
        visible,
        embedding,
        match_weight,
        layer_gains,
        joint_weight,
        output_weight,
        expand_weight,
        reduce_weight,
    )
    by_track = exchange(crossed)
    tracked = pl.pallas_call(
        lambda *refs: track_kernel(per_device, *refs),
        out_shape=jax.ShapeDtypeStruct((devices, pad_rows, LANES), BF16),
        in_specs=[vmem] * 7,
        out_specs=vmem,
        scratch_shapes=[pltpu.VMEM((devices * pad_rows, LANES), F32)],
        name="track_block",
    )(by_track, visible, layer_gains, joint_weight, output_weight, expand_weight, reduce_weight)
    arrived = exchange(tracked)
    return pl.pallas_call(
        layout_kernel,
        out_shape=jax.ShapeDtypeStruct((1, points, features), BF16),
        in_specs=[vmem],
        out_specs=vmem,
        scratch_shapes=[pltpu.VMEM((devices * pad_rows, LANES), F32)],
        name="layout",
    )(arrived)


def solution(mesh):
    placed = (
        P("frame", "groups", None, None),
        P("frame", "groups"),
        P("frame", "groups"),
        P("groups"),
        P(None, "groups"),
        P("groups"),
        P(),
        P(),
        P(),
        P(),
        P(),
        P(),
    )
    return jax.shard_map(
        shards, mesh=mesh, in_specs=placed, out_specs=P("frame", "groups", None), check_vma=False
    )
```

time: 185 us -> 70.9 us (0.38)
  local copies, waits for them, and re-layouts: 92.9 us -> 0.71 us
  blocking collectives: 52.5 us -> 22.9 us
  Pallas kernels: 0 us -> 25.7 us
  matrix products: 11.6 us -> 0 us
  other arithmetic: 13.9 us -> 3.09 us
  starting transfers between devices: 4.41 us -> 7.56 us
    gather x8 -> x0, local copies, waits for them, and re-layouts: 79.1 us -> none  [take_rows(): one_map[one_index]]
    psum x1 -> x0, blocking collectives: 43 us -> none  [shards(): fine_feat, coarse_feat = lax.psum((fine_term, coarse_term), 'frame')]
    pallas_call x0 -> x4, Pallas kernels: none -> 25.7 us  [the longest x1 13.9 us: shards(): pl.pallas_call(lambda *refs: frame_kernel(slots, *refs), out_shape=jax.Sh...]
    all_to_all x1 -> x2, blocking collectives: 9.48 us -> 22.9 us  [exchange(): lax.all_to_all(block, 'frame', split_axis=0, concat_axis=0, tiled=True)]
    dot_general x13 -> x0, matrix products: 11.2 us -> none  [the longest x2 4.76 us: finish(): jnp.einsum('abe,ed->abd', widened, reduce_weight, preferred_element_type=...]
    reduce_sum x5 -> x2, other arithmetic: 7.63 us -> 1.08 us  [the longest x1 0.92 us: shards(): load = jnp.sum(query_frame[:, None] == jnp.arange(devices)[None, :], axis=0)]
    another operation x2 -> x0, local copies, waits for them, and re-layouts: 6.19 us -> none
    all_to_all x1, starting transfers between devices: 4.41 us -> 7.56 us  [exchange(): lax.all_to_all(block, 'frame', split_axis=0, concat_axis=0, tiled=True)]
  transfers between devices with their start and end apart: 1 -> 1, of which waited for: 1 -> 1; matrix products, arithmetic and copies ran while one was open for 0% -> 1% of each run, Pallas kernels for 0% -> 0%
where the time goes in v1:
time: 70.9 us; the launch traced here: 70.6 us
  Pallas kernels  25.7 us (36%)
  blocking collectives  22.9 us (32%)
  waiting for transfers between devices  9.22 us (13%)
  starting transfers between devices  7.56 us (11%)
  other arithmetic  3.09 us (4%)
  between operations  1.41 us (2%)
  local copies, waits for them, and re-layouts  0.71 us (1%)
    all_to_all x2, blocking collectives, exchange(): lax.all_to_all(block, 'frame', split_axis=0, concat_axis=0, tiled=True)  22.9 us
    pallas_call x1, Pallas kernels, shards(): pl.pallas_call(lambda *refs: frame_kernel(slots, *refs), out_shape=jax.Sh...  13.9 us
    all_to_all x1, waiting for transfers between devices, exchange(): lax.all_to_all(block, 'frame', split_axis=0, concat_axis=0, tiled=True)  9.22 us
    all_to_all x1, starting transfers between devices, exchange(): lax.all_to_all(block, 'frame', split_axis=0, concat_axis=0, tiled=True)  7.56 us
    pallas_call x1, Pallas kernels, shards(): pl.pallas_call(lambda *refs: track_kernel(per_device, *refs), out_shape=j...  5.9 us
    pallas_call x1, Pallas kernels, send_round(): pack(which.reshape(1), query_row, pixel_row, pixel_column, feature_map)  4.33 us
    pallas_call x1, Pallas kernels, shards(): pl.pallas_call(layout_kernel, out_shape=jax.ShapeDtypeStruct((1, points,...  1.63 us
  transfers between devices with their start and end apart: 1, of which 1 were waited for; matrix products, arithmetic and copies ran while one was open for 1% of the time, Pallas kernels for 0%

profile of v1, /device:TPU:0, one launch (start us, length us, event | category | flops | bytes accessed | tf_op | source)
XLA Modules:
  0.0 70.6 jit_solution(6913074730798791404)
XLA Ops:
  0.0 0.0 copy-start.4
  0.0 0.0 copy-start
  0.0 0.0 copy-start.2
  0.0 0.0 copy-start.3
  0.0 0.9 %convert_reduce_fusion = s32[32]{0:T(128)S(1)} fusion(s32[128]{0:T(128)} %param.17), kind=kLoop, calls=%fused_computation.15 | loop fusion | flops 12256 | bytes 640 | tf_op jit(solution)/shard_map/reduce_sum | solution.py:372
  0.9 0.6 reduce_max.9
  2.2 0.7 convert_bitcast_fusion
  2.9 0.2 select_reduce_fusion
  3.1 4.3 %pack.7 = bf16[32,16,256]{2,1,0:T(8,128)(2,1)} custom-call(s32[1]{0:T(128)} %constant.67.clone.1.refs_0_, s32[1,128]{1,0:T(1,128)} %bitcast.23, s32[1,128]{1,0:T(1,128)} %refs_0_.1, s32[1,128]{1,0:T(1,128)} %refs_1_.2, bf16[1,64,128,128]{3,2,1,0:T(8,128)(2,1)} %refs_5_.2), custom_call_target="tpu_custom_call" | custom-call | tf_op jit(solution)/shard_map/pack/pallas_call | solution.py:369
  7.4 0.0 copy-done.4
  7.4 0.0 copy-done
  7.4 0.0 copy-done.2
  7.5 0.0 copy-done.3
  7.5 7.6 %all-to-all-start.1 = ((bf16[32,16,256]{2,1,0:T(8,128)(2,1)}), bf16[32,16,256]{2,1,0:T(8,128)(2,1)S(1)}, u32[]{:S(2)}, u32[]{:S(2)}) async-start(bf16[32,16,256]{2,1,0:T(8,128)(2,1)} %pack.7), calls=%async_computation.1 | async-start | bytes 524288 | tf_op jit(solution)/shard_map/all_to_all | solution.py:366
  15.7 0.1 fusion.8
  15.8 0.6 pad_maximum_fusion.refs_7_
  16.4 9.2 %all-to-all-done.1.refs_3_ = bf16[32,16,256]{2,1,0:T(8,128)(2,1)S(1)} async-done(((bf16[32,16,256]{2,1,0:T(8,128)(2,1)}), bf16[32,16,256]{2,1,0:T(8,128)(2,1)S(1)}, u32[]{:S(2)}, u32[]{:S(2)}) %all-to-all-start.1) | async-done | bytes 262176 | tf_op jit(solution)/shard_map/all_to_all | solution.py:366
  25.6 0.0 copy-start.1
  25.6 0.7 copy-done.1
  26.3 13.9 %frame_block.1 = bf16[32,16,128]{2,1,0:T(8,128)(2,1)} custom-call(s32[1,128]{1,0:T(1,128)S(1)} %get-tuple-element.309, s32[1,128]{1,0:T(1,128)S(1)} %get-tuple-element.310, s32[1,128]{1,0:T(1,128)S(1)} %get-tuple-element.311, bf16[32,16,256]{2,1,0:T(8,128)(2,1)} %copy-done.1, bf16[128,256]{1,0:T(8,128)(2,1)S(1)} %get-tuple-element.192.refs_4_, ...), custom_call_target="tpu_custom_call" | custom-call | tf_op jit(solution)/shard_map/frame_block/pallas_call | solution.py:385
  40.2 11.5 %all_to_all.26.refs_0_ = bf16[32,16,128]{2,1,0:T(8,128)(2,1)} all-to-all(bf16[32,16,128]{2,1,0:T(8,128)(2,1)} %frame_block.1), channel_id=1, replica_groups=mesh['groups'=1,'frame'=32] {'frame'}, dimensions={0} | all-to-all | bytes 262144 | tf_op jit(solution)/shard_map/all_to_all | solution.py:366
  51.6 5.9 %track_block.1 = bf16[32,16,128]{2,1,0:T(8,128)(2,1)} custom-call(bf16[32,16,128]{2,1,0:T(8,128)(2,1)} %all_to_all.26.refs_0_, s32[32,128]{1,0:T(8,128)} %refs_1_.3, f32[2,2,384]{2,1,0:T(2,128)} %refs_2_.3, bf16[2,384,1152]{2,1,0:T(8,128)(2,1)} %refs_3_.3, bf16[2,384,384]{2,1,0:T(8,128)(2,1)} %refs_4_.3, bf16[2,384,1536]{2,1,0:T(8,128)(2,1)} %refs_5_.3, ...), custom_call_target="tpu_custom_call" | custom-call | tf_op jit(solution)/shard_map/track_block/pallas_call | solution.py:414
  57.5 11.5 %all_to_all.27.received_ref = bf16[32,16,128]{2,1,0:T(8,128)(2,1)} all-to-all(bf16[32,16,128]{2,1,0:T(8,128)(2,1)} %track_block.1), channel_id=1, replica_groups=mesh['groups'=1,'frame'=32] {'frame'}, dimensions={0} | all-to-all | bytes 262144 | tf_op jit(solution)/shard_map/all_to_all | solution.py:366
  69.0 1.6 %layout.1 = bf16[1,128,384]{2,1,0:T(8,128)(2,1)} custom-call(bf16[32,16,128]{2,1,0:T(8,128)(2,1)} %all_to_all.27.received_ref), custom_call_target="tpu_custom_call" | custom-call | tf_op jit(solution)/shard_map/layout/pallas_call | solution.py:423
  (3 shorter events, 0.0 us)
Async XLA Ops:
  0.0 7.4 %copy-start.4 = (s32[128]{0:T(128)S(1)}, s32[128]{0:T(128)}, u32[]{:S(2)}) copy-start(s32[128]{0:T(128)} %param.17) | copy-start | bytes 1540
  0.0 7.4 %copy-start = (bf16[1,64,128,128]{3,2,1,0:T(8,128)(2,1)S(1)}, bf16[1,64,128,128]{3,2,1,0:T(8,128)(2,1)}, u32[]{:S(2)}) copy-start(bf16[1,64,128,128]{3,2,1,0:T(8,128)(2,1)} %refs_5_.2) | copy-start | bytes 6291460
  0.0 7.4 %copy-start.2 = (s32[1,128]{1,0:T(1,128)S(1)}, s32[1,128]{1,0:T(1,128)}, u32[]{:S(2)}) copy-start(s32[1,128]{1,0:T(1,128)} %refs_0_.1) | copy-start | bytes 1540
  0.0 7.5 %copy-start.3 = (s32[1,128]{1,0:T(1,128)S(1)}, s32[1,128]{1,0:T(1,128)}, u32[]{:S(2)}) copy-start(s32[1,128]{1,0:T(1,128)} %refs_1_.2) | copy-start | bytes 1540
  7.5 18.1 %all-to-all-start.1 = ((bf16[32,16,256]{2,1,0:T(8,128)(2,1)}), bf16[32,16,256]{2,1,0:T(8,128)(2,1)S(1)}, u32[]{:S(2)}, u32[]{:S(2)}) async-start(bf16[32,16,256]{2,1,0:T(8,128)(2,1)} %pack.7), calls=%async_computation.1 | async-start | bytes 524288 | tf_op jit(solution)/shard_map/all_to_all | solution.py:366
  25.6 0.7 copy-start.1

commit v2 on v1

v2 whole, which is shorter than its diff:
```python
import math

import jax
import jax.numpy as jnp
from jax import lax
from jax.experimental import pallas as pl
from jax.experimental.pallas import tpu as pltpu
from jax.sharding import PartitionSpec as P

HEADS = 8
PATCH = 7
EPSILON = 1e-05
LANES = 128
TILE = 16
SPAN = 64
MIB = 1 << 20
F32 = jnp.float32
BF16 = jnp.bfloat16
VMEM = pltpu.MemorySpace.VMEM
SMEM = pltpu.MemorySpace.SMEM


def normalize(values, weights):
    average = jnp.mean(values, axis=-1, keepdims=True)
    centred = values - average
    variance = jnp.mean(centred * centred, axis=-1, keepdims=True)
    return centred * lax.rsqrt(variance + EPSILON) * weights


def iota(shape, axis):
    return lax.broadcasted_iota(jnp.int32, shape, axis)


def matmul(left, right):
    return jnp.dot(left, right, preferred_element_type=F32)


def matmul_nt(left, right):
    return lax.dot_general(left, right, (((1,), (1,)), ((), ())), preferred_element_type=F32)


def pack(slots, base, query, row, column, copies, cells, out_ref):
    me = lax.axis_index("frame")
    points = query.shape[1]
    chunks, depth, breadth, channels = cells.shape
    mine = query == me
    before = jnp.where(iota((points, points), 0) < iota((points, points), 1), 1.0, 0.0).astype(BF16)
    rank = matmul(jnp.broadcast_to(jnp.where(mine, 1.0, 0.0), (8, points)).astype(BF16), before)[:1]
    slot = jnp.where(mine, rank.astype(jnp.int32) - base, -1)
    rows = block_rows(slots)
    line = iota((rows, points), 0)
    held = jnp.where(line < slots, line, line - slots) == jnp.where(slot < slots, slot, -1)

    def gathered(values):
        return jnp.sum(jnp.where(held, values + 1, 0).astype(F32), axis=1, keepdims=True).astype(jnp.int32) - 1

    fine_at = gathered(row * breadth + column)
    coarse_at = gathered((row >> 1) * (breadth // 2) + (column >> 1))
    is_fine = iota((rows, 1), 0) < slots
    wanted = jnp.where(is_fine, fine_at, coarse_at)
    size = depth * breadth
    place = iota((1, size), 1)
    coarse_place = (place // breadth >> 1) * (breadth // 2) + (place % breadth >> 1)
    both_places = jnp.where(is_fine, place, coarse_place)
    weight = jnp.where(is_fine, 1.0, 0.25)
    total = None
    for chunk in range(chunks):
        start = jnp.where(is_fine, chunk * size, chunk * size // 4)
        chosen = jnp.where(both_places == wanted - start, weight, 0.0).astype(BF16)
        copies[chunk].wait()
        part = matmul(chosen, cells[chunk].reshape(size, channels))
        total = part if total is None else total + part
    twice = jnp.concatenate([total, total], axis=0).astype(BF16)
    for pair in range(out_ref.shape[0] // (2 * rows)):
        out_ref[pair * 2 * rows : (pair + 1) * 2 * rows, :] = twice


def map_copies(map_ref, cells, sems):
    chunks, depth, _, _ = cells.shape
    copies = [
        pltpu.make_async_copy(map_ref.at[0, pl.ds(chunk * depth, depth)], cells.at[chunk], sems.at[chunk])
        for chunk in range(chunks)
    ]
    for copy in copies:
        copy.start()
    return copies


def pack_again_kernel(slots, round_ref, query_ref, row_ref, column_ref, map_ref, out_ref, cells, sems):
    copies = map_copies(map_ref, cells, sems)
    pack(slots, round_ref[0] * slots, query_ref[...], row_ref[...], column_ref[...], copies, cells, out_ref)


def unpack_again_kernel(slots, devices, round_ref, query_ref, received_ref, before_ref, out_ref):
    chosen = choose(query_ref[...], devices, slots, round_ref[0] * slots)
    out_ref[...] = before_ref[...] + matmul(chosen, received_ref[...]).astype(BF16)


def block_rows(slots):
    return 8 * -(-2 * slots // 8)


def choose(query_row, devices, slots, base):
    points = query_row.shape[1]
    across = jnp.broadcast_to(query_row.astype(F32), (points, points))
    down = across.T
    earlier = (across == down) & (iota((points, points), 1) < iota((points, points), 0))
    rank = jnp.sum(jnp.where(earlier, 1.0, 0.0), axis=1, keepdims=True).astype(jnp.int32)
    frame = down[:, :1].astype(jnp.int32)
    rows = block_rows(slots)
    inside = (rank >= base) & (rank < base + slots)
    fine_at = jnp.where(inside, frame * rows + rank - base, -1)
    coarse_at = jnp.where(inside, frame * rows + slots + rank - base, -1)
    place = iota((points, devices * rows), 1)
    chosen = [jnp.where(place == at, 1.0, 0.0).astype(BF16) for at in (fine_at, coarse_at)]
    return jnp.concatenate(chosen, axis=0)


def prepare_kernel(
    slots,
    row_ref,
    column_ref,
    window_ref,
    query_ref,
    row_line_ref,
    column_line_ref,
    match_ref,
    map_ref,
    packed_ref,
    rounds_ref,
    chosen_ref,
    fine_ref,
    coarse_ref,
    spread_ref,
    embedding_ref,
    cells,
    fine_map,
    coarse_map,
    match,
    sems,
    match_sem,
):
    match_copy = pltpu.make_async_copy(match_ref, match, match_sem)
    match_copy.start()
    copies = map_copies(map_ref, cells, sems)
    me = lax.axis_index("frame")
    points = query_ref.shape[1]
    _, height, breadth, channels = map_ref.shape
    depth = cells.shape[1]
    half = breadth // 2
    rows = block_rows(slots)
    devices = packed_ref.shape[0] // rows
    query = query_ref[...]
    chosen_ref[...] = choose(query, devices, slots, 0)
    there = jnp.where(iota((devices, points), 0) == query, 1.0, 0.0)
    load = jnp.max(jnp.sum(there, axis=1, keepdims=True)).astype(jnp.int32)
    rounds_ref[0] = (load + slots - 1) // slots
    place = iota((2 * SPAN, match_ref.shape[0]), 0)
    level, k, m = place // SPAN, place % SPAN // 8, place % 8
    wanted = jnp.where((k < PATCH) & (m < PATCH), (level * PATCH + k) * PATCH + m, -1)
    pick = jnp.where(iota(place.shape, 1) == wanted, 1.0, 0.0).astype(BF16)
    match_copy.wait()
    spread_ref[...] = matmul(pick, match[...]).astype(BF16)
    features = embedding_ref.shape[1]
    feature = iota((1, features), 1)
    of_sine = feature < features // 2
    step = jnp.where(of_sine, feature, feature - features // 2).astype(F32)
    angle = (window_ref[0] + me).astype(F32) * jnp.exp(-math.log(10000.0) * step / (features // 2))
    embedding_ref[...] = jnp.where(of_sine, jnp.sin(angle), jnp.cos(angle))
    pack(slots, 0, query, row_line_ref[...], column_line_ref[...], copies, cells, packed_ref)
    pool = jnp.where(
        iota((half, 2 * breadth), 1) % breadth // 2 == iota((half, 2 * breadth), 0), 0.25, 0.0
    ).astype(BF16)
    coarse_map[pl.ds(height // 2 * half, 8), :] = jnp.zeros((8, channels), F32)

    def convert(pair, carry):
        both = cells.reshape(height * breadth, channels)[
            pl.ds(pl.multiple_of(pair * 2 * breadth, 2 * breadth), 2 * breadth), :
        ]
        fine_map[pl.ds(pl.multiple_of(pair * 2 * breadth, 2 * breadth), 2 * breadth), :] = both.astype(F32)
        coarse_map[pl.ds(pl.multiple_of(pair * half, half), half), :] = matmul(pool, both).astype(BF16).astype(F32)
        return carry

    lax.fori_loop(0, height // 2, convert, 0, unroll=4)
    blank = jnp.zeros((8, channels), F32)

    def gather(point, carry):
        row, column = row_ref[0, point], column_ref[0, point]
        for ref, out, wide, at in (
            (fine_map, fine_ref, breadth, row * breadth + column - (3 * breadth + 3)),
            (coarse_map, coarse_ref, half, (row >> 1) * half + (column >> 1) - (3 * half + 3)),
        ):
            window = ref.at[pl.ds(at, 6 * wide + 8), :]
            target = out.at[pl.ds(pl.multiple_of(point * SPAN, SPAN), SPAN), :]
            lines = [window[k * wide : k * wide + 8, :] for k in range(PATCH)] + [blank]
            for t in range(4):
                target[t * TILE : (t + 1) * TILE, :] = jnp.concatenate(lines[2 * t : 2 * t + 2], axis=0).astype(BF16)
        return carry

    lax.fori_loop(0, points, gather, 0, unroll=8)


def attention(queries, keyset, values, permitted):
    rows, features = queries.shape
    per_head = features // HEADS
    head_of = iota((1, features), 1) // per_head
    spread = jnp.concatenate(
        [jnp.where(head_of == head, queries, 0) for head in range(HEADS)], axis=0
    )
    scores = matmul_nt(spread, keyset) * (1.0 / math.sqrt(per_head))
    outcome = None
    parts = []
    for head in range(HEADS):
        part = jnp.where(permitted, scores[head * rows : (head + 1) * rows], -1e30)
        part = jnp.exp(part - jnp.max(part, axis=-1, keepdims=True))
        parts.append((part / jnp.sum(part, axis=-1, keepdims=True)).astype(BF16))
    mixed = matmul(jnp.concatenate(parts, axis=0), values)
    for head in range(HEADS):
        term = jnp.where(head_of == head, mixed[head * rows : (head + 1) * rows], 0.0)
        outcome = term if outcome is None else outcome + term
    return outcome.astype(BF16)


def finish(stream, attended, gain, output_weight, expand_weight, reduce_weight):
    stream = stream + matmul(attended, output_weight)
    hidden = normalize(stream, gain).astype(BF16)
    widened = jax.nn.gelu(matmul(hidden, expand_weight), approximate=True).astype(BF16)
    return stream + matmul(widened, reduce_weight)


def frame_kernel(
    extra_ref,
    received_ref,
    chosen_ref,
    fine_ref,
    coarse_ref,
    spread_ref,
    embedding_ref,
    visible_ref,
    gains_ref,
    joint_ref,
    output_ref,
    expand_ref,
    reduce_ref,
    out_ref,
    staged,
):
    me = lax.axis_index("frame")
    points = visible_ref.shape[1]
    channels = received_ref.shape[1]
    features = spread_ref.shape[1]
    devices, pad_rows, _ = out_ref.shape
    anchors = matmul(chosen_ref[...], received_ref[...]).astype(BF16)
    if extra_ref is not None:
        anchors = anchors + extra_ref[...]
    line, lane = iota((8, LANES), 0), iota((8, LANES), 1)
    rows = []
    for start in range(0, points, TILE):
        levels = []
        for level, ref in enumerate((fine_ref, coarse_ref)):
            some = anchors[level * points + start : level * points + start + TILE]
            levels.append(matmul_nt(some, ref[start * SPAN : (start + TILE) * SPAN, :]))
        for part in range(2):
            sides = []
            for level, scores in enumerate(levels):
                own = scores[part * 8 : part * 8 + 8, part * 8 * SPAN : (part + 1) * 8 * SPAN]
                kept = own[:, :LANES]
                for index in range(1, 4):
                    kept = jnp.where(line // 2 == index, own[:, index * LANES : (index + 1) * LANES], kept)
                sides.append(jnp.where(line % 2 == level, kept, pltpu.roll(kept, SPAN, 1)))
            rows.append(jnp.where(lane < SPAN, sides[0], sides[1]))
    matches = (jnp.concatenate(rows, axis=0) * (1.0 / math.sqrt(channels))).astype(BF16)
    tokens = (matmul(matches, spread_ref[...]) + embedding_ref[...]).astype(BF16)

    stream = tokens.astype(F32)
    hidden = normalize(stream, gains_ref[0, 0:1, :]).astype(BF16)
    projected = matmul(hidden, joint_ref[0]).astype(BF16)
    allowed = visible_ref[pl.ds(me, 1), :] == 1
    permitted = allowed | (iota((points, points), 0) == iota((points, points), 1))
    attended = attention(
        projected[:, :features], projected[:, features : 2 * features], projected[:, 2 * features :], permitted
    )
    crossed = finish(stream, attended, gains_ref[0, 1:2, :], output_ref[0], expand_ref[0], reduce_ref[0])
    chunks = features // LANES
    for i in range(points // devices):
        for c in range(chunks):
            staged[pl.ds(i * chunks + c, devices, stride=pad_rows), :] = crossed[
                i * devices : (i + 1) * devices, c * LANES : (c + 1) * LANES
            ]
    out_ref[...] = staged[...].astype(BF16).reshape(out_ref.shape)


def track_kernel(
    per_device,
    received_ref,
    visible_ref,
    gains_ref,
    joint_ref,
    output_ref,
    expand_ref,
    reduce_ref,
    out_ref,
    staged,
):
    me = lax.axis_index("frame")
    length, pad_rows, _ = received_ref.shape
    features = output_ref.shape[1]
    chunks = features // LANES
    points = visible_ref.shape[1]
    devices = out_ref.shape[0]
    half_way = length // 2
    staged[...] = received_ref[...].reshape(length * pad_rows, LANES).astype(F32)
    stream = jnp.concatenate(
        [
            jnp.concatenate(
                [staged[pl.ds(i * chunks + c, length, stride=pad_rows), :] for c in range(chunks)], axis=1
            )
            for i in range(per_device)
        ],
        axis=0,
    )
    total = per_device * length
    hidden = normalize(stream, gains_ref[1, 0:1, :]).astype(BF16)
    projected = matmul(hidden, joint_ref[1]).astype(BF16)

    def later(array):
        return jnp.concatenate(
            [array[i * length + half_way : (i + 1) * length] for i in range(per_device)], axis=0
        )

    rest = length - half_way
    lane = iota((points, total), 1)
    pick = jnp.where(iota((points, total), 0) == lane // length * devices + me, 1.0, 0.0).astype(BF16)
    seen = matmul(jnp.where(visible_ref[...] == 1, 1.0, 0.0).astype(BF16), pick)
    seen = jnp.where(iota((length, total), 1) % length == iota((length, total), 0), seen, 0.0)
    allowed = jnp.sum(seen, axis=0, keepdims=True) > 0.5
    query_at = iota((per_device * rest, total), 0)
    key_at = iota((per_device * rest, total), 1)
    same_point = query_at // rest == key_at // length
    same_frame = query_at % rest + half_way == key_at % length
    permitted = same_point & (allowed | same_frame)
    attended = attention(
        later(projected[:, :features]),
        projected[:, features : 2 * features],
        projected[:, 2 * features :],
        permitted,
    )
    tracked = finish(later(stream), attended, gains_ref[1, 1:2, :], output_ref[1], expand_ref[1], reduce_ref[1])
    for i in range(per_device):
        for c in range(chunks):
            piece = tracked[i * rest : (i + 1) * rest, c * LANES : (c + 1) * LANES]
            at = i * chunks + c
            staged[pl.ds(at, rest, stride=pad_rows), :] = piece
            staged[pl.ds(rest * pad_rows + at, half_way, stride=pad_rows), :] = jnp.broadcast_to(
                piece[rest - 1 :], (half_way, LANES)
            )
    out_ref[...] = staged[...].astype(BF16).reshape(out_ref.shape)


def layout_kernel(received_ref, out_ref, staged):
    devices, pad_rows, _ = received_ref.shape
    _, points, features = out_ref.shape
    chunks = features // LANES
    staged[...] = received_ref[...].reshape(devices * pad_rows, LANES).astype(F32)
    for i in range(points // devices):
        for c in range(chunks):
            out_ref[0, i * devices : (i + 1) * devices, c * LANES : (c + 1) * LANES] = staged[
                pl.ds(i * chunks + c, devices, stride=pad_rows), :
            ].astype(BF16)


def exchange(block):
    return lax.all_to_all(block, "frame", split_axis=0, concat_axis=0, tiled=True)


def step(
    further,
    feature_map,
    pixel_row,
    pixel_column,
    query_frame,
    visible,
    window_start,
    match_weight,
    layer_gains,
    *weights,
):
    _, height, breadth, channels = feature_map.shape
    points = query_frame.shape[0]
    features = match_weight.shape[1]
    devices = lax.axis_size("frame")
    per_device = points // devices
    slots = 3 * per_device
    rows = block_rows(slots)
    pad_rows = TILE * -(-per_device * (features // LANES) // TILE)
    query_row = query_frame.reshape(1, points)
    vmem = pl.BlockSpec(memory_space=VMEM)
    smem = pl.BlockSpec(memory_space=SMEM)
    here = pl.BlockSpec(memory_space=pltpu.MemorySpace.HBM)
    chunks = 8
    map_scratch = pltpu.VMEM((chunks, height // chunks, breadth, channels), BF16)
    map_sems = pltpu.SemaphoreType.DMA((chunks,))
    block = jax.ShapeDtypeStruct((devices * rows, channels), BF16)

    packed, rounds, *prepared = pl.pallas_call(
        lambda *refs: prepare_kernel(slots, *refs),
        out_shape=[
            block,
            jax.ShapeDtypeStruct((1,), jnp.int32),
            jax.ShapeDtypeStruct((2 * points, devices * rows), BF16),
            jax.ShapeDtypeStruct((points * SPAN, channels), BF16),
            jax.ShapeDtypeStruct((points * SPAN, channels), BF16),
            jax.ShapeDtypeStruct((2 * SPAN, features), BF16),
            jax.ShapeDtypeStruct((1, features), F32),
        ],
        in_specs=[smem, smem, smem, vmem, vmem, vmem, here, here],
        out_specs=[vmem, smem] + [vmem] * 5,
        scratch_shapes=[
            map_scratch,
            pltpu.VMEM((height * breadth, channels), F32),
            pltpu.VMEM((height * breadth // 4 + 8, channels), F32),
            pltpu.VMEM(match_weight.shape, BF16),
            map_sems,
            pltpu.SemaphoreType.DMA,
        ],
        compiler_params=pltpu.CompilerParams(vmem_limit_bytes=(16 + points // 16) * MIB),
        name="prepare",
    )(
        pixel_row,
        pixel_column,
        window_start,
        query_row,
        pixel_row,
        pixel_column,
        match_weight,
        feature_map,
    )
    rounds = rounds.reshape(())
    received = exchange(packed)
    extra = ()
    if further:

        def next_round(state):
            which, extra = state
            again = pl.pallas_call(
                lambda *refs: pack_again_kernel(slots, *refs),
                out_shape=block,
                in_specs=[smem, vmem, vmem, vmem, here],
                out_specs=vmem,
                scratch_shapes=[map_scratch, map_sems],
                compiler_params=pltpu.CompilerParams(vmem_limit_bytes=8 * MIB),
                name="pack_again",
            )(which.reshape(1), query_row, pixel_row, pixel_column, feature_map)
            extra = pl.pallas_call(
                lambda *refs: unpack_again_kernel(slots, devices, *refs),
                out_shape=jax.ShapeDtypeStruct(extra.shape, BF16),
                in_specs=[smem, vmem, vmem, vmem],
                out_specs=vmem,
                compiler_params=pltpu.CompilerParams(vmem_limit_bytes=(4 + points // 16) * MIB),
                name="unpack_again",
            )(which.reshape(1), query_row, exchange(again), extra)
            return which + 1, extra

        received, rounds = lax.optimization_barrier((received, lax.pmax(rounds, "groups")))
        start = (jnp.int32(1), jnp.zeros((2 * points, channels), BF16))
        extra = lax.while_loop(lambda state: state[0] < rounds, next_round, start)[1:]
    crossed = pl.pallas_call(
        frame_kernel if further else lambda *refs: frame_kernel(None, *refs),
        out_shape=jax.ShapeDtypeStruct((devices, pad_rows, LANES), BF16),
        in_specs=[vmem] * (12 + len(extra)),
        out_specs=vmem,
        scratch_shapes=[pltpu.VMEM((devices * pad_rows, LANES), F32)],
        compiler_params=pltpu.CompilerParams(vmem_limit_bytes=(8 + points // 16) * MIB),
        name="frame_block",
    )(*extra, received, *prepared, visible, layer_gains, *weights)
    by_track = exchange(crossed)
    tracked = pl.pallas_call(
        lambda *refs: track_kernel(per_device, *refs),
        out_shape=jax.ShapeDtypeStruct((devices, pad_rows, LANES), BF16),
        in_specs=[vmem] * 7,
        out_specs=vmem,
        scratch_shapes=[pltpu.VMEM((devices * pad_rows, LANES), F32)],
        compiler_params=pltpu.CompilerParams(vmem_limit_bytes=(4 + points // 16) * MIB),
        name="track_block",
    )(by_track, visible, layer_gains, *weights)
    arrived = exchange(tracked)
    handed = pl.pallas_call(
        layout_kernel,
        out_shape=jax.ShapeDtypeStruct((1, points, features), BF16),
        in_specs=[vmem],
        out_specs=vmem,
        scratch_shapes=[pltpu.VMEM((devices * pad_rows, LANES), F32)],
        compiler_params=pltpu.CompilerParams(vmem_limit_bytes=4 * MIB),
        name="layout",
    )(arrived)
    return rounds, handed


def shards(*arrays):
    rounds, handed = step(False, *arrays)

    def again(state):
        rounds, _ = state
        return jnp.int32(1), step(True, *lax.optimization_barrier((rounds,) + arrays)[1:])[1]

    return lax.while_loop(lambda state: state[0] > 1, again, (lax.pmax(rounds, "groups"), handed))[1]


def solution(mesh):
    placed = (
        P("frame", "groups", None, None),
        P("frame", "groups"),
        P("frame", "groups"),
        P("groups"),
        P(None, "groups"),
        P("groups"),
        P(),
        P(),
        P(),
        P(),
        P(),
        P(),
    )
    return jax.shard_map(
        shards, mesh=mesh, in_specs=placed, out_specs=P("frame", "groups", None), check_vma=False
    )
```

time: 70.9 us -> 55 us (0.78)
  blocking collectives: 22.9 us -> 36.7 us
  Pallas kernels: 25.7 us -> 16.2 us
  waiting for transfers between devices: 9.22 us -> 0 us
  starting transfers between devices: 7.56 us -> 0 us
  other arithmetic: 3.09 us -> 0 us
  loops' own time: 0.01 us -> 0.82 us
    all_to_all x2 -> x3, blocking collectives: 22.9 us -> 36.7 us  [exchange(): lax.all_to_all(block, 'frame', split_axis=0, concat_axis=0, tiled=True)]
    pallas_call x4, Pallas kernels: 25.7 us -> 16.2 us  [the longest x1 6.89 us: step(): pl.pallas_call(lambda *refs: prepare_kernel(slots, *refs), out_shape=[blo...]
    all_to_all x1 -> x0, waiting for transfers between devices: 9.22 us -> none  [exchange(): lax.all_to_all(block, 'frame', split_axis=0, concat_axis=0, tiled=True)]
    all_to_all x1 -> x0, starting transfers between devices: 7.56 us -> none  [exchange(): lax.all_to_all(block, 'frame', split_axis=0, concat_axis=0, tiled=True)]
    reduce_sum x2 -> x0, other arithmetic: 1.08 us -> none  [the longest x1 0.92 us: shards(): load = jnp.sum(query_frame[:, None] == jnp.arange(devices)[None, :], axis=0)]
    another operation x1, loops' own time: 0.01 us -> 0.82 us  [shards(): lax.while_loop(lambda state: state[0] > 1, again, (lax.pmax(rounds, 'grou...]
  transfers between devices with their start and end apart: 1 -> 0, of which waited for: 1 -> 0; matrix products, arithmetic and copies ran while one was open for 1% -> 0% of each run, Pallas kernels for 0% -> 0%
where the time goes in v2:
time: 55 us; the launch traced here: 54.8 us
  blocking collectives  36.7 us (67%)
  Pallas kernels  16.2 us (29%)
  between operations  1.06 us (2%)
  loops' own time  0.82 us (1%)
    all_to_all x3, blocking collectives, exchange(): lax.all_to_all(block, 'frame', split_axis=0, concat_axis=0, tiled=True)  36.7 us
    pallas_call x1, Pallas kernels, step(): pl.pallas_call(lambda *refs: prepare_kernel(slots, *refs), out_shape=[blo...  6.89 us
    pallas_call x1, Pallas kernels, step(): pl.pallas_call(frame_kernel if further else lambda *refs: frame_kernel(No...  6.51 us
    pallas_call x1, Pallas kernels, step(): pl.pallas_call(lambda *refs: track_kernel(per_device, *refs), out_shape=j...  2.09 us

profile of v2, /device:TPU:0, one launch (start us, length us, event | category | flops | bytes accessed | tf_op | source)
XLA Modules:
  0.0 54.8 jit_solution(8911112214255051022)
XLA Ops:
  0.0 0.0 copy-start.11
  0.0 0.0 copy-start.13
  0.0 0.0 copy-start.2
  0.8 6.9 %prepare.3 = (bf16[768,128]{1,0:T(8,128)(2,1)S(1)}, s32[1]{0:T(128)}, bf16[256,768]{1,0:T(8,128)(2,1)S(1)}, bf16[8192,128]{1,0:T(8,128)(2,1)S(1)}, bf16[8192,128...) custom-call(s32[1,128]{1,0:T(1,128)} %refs_4_.2, s32[1,128]{1,0:T(1,128)} %refs_5_.2, ...), custom_call_target="tpu_custom_call" | custom-call | tf_op jit(solution)/shard_map/prepare/pallas_call | solution.py:405
  7.7 16.1 %all_to_all.50 = bf16[32,24,128]{2,1,0:T(8,128)(2,1)S(1)} all-to-all(bf16[32,24,128]{2,1,0:T(8,128)(2,1)S(1)} %bitcast.20), channel_id=1, replica_groups=mesh['groups'=1,'frame'=32] {'frame'}, dimensions={0} | all-to-all | bytes 393216 | tf_op jit(solution)/shard_map/all_to_all | solution.py:373
  23.8 0.0 copy-done.11
  23.8 0.0 copy-done.13
  23.8 0.0 copy-done.2
  23.8 0.0 copy-start.4
  23.8 0.0 copy-start.6
  23.8 0.0 copy-start.8
  23.8 6.5 %frame_block.3 = bf16[32,16,128]{2,1,0:T(8,128)(2,1)S(1)} custom-call(bf16[768,128]{1,0:T(8,128)(2,1)S(1)} %bitcast.19, bf16[256,768]{1,0:T(8,128)(2,1)S(1)} %get-tuple-element.143.refs_1_, bf16[8192,128]{1,0:T(8,128)(2,1)S(1)} %get-tuple-element.144.refs_2_, bf16[8192,128]{1,0:T(8,128)(2,1)S(1)} %get-tuple-element.145.refs_3_, ...), custom_call_target="tpu_custom_call" | custom-call | tf_op jit(solution)/shard_map/frame_block/pallas_call | solution.py:467
  30.4 10.6 %all_to_all.51.refs_0_ = bf16[32,16,128]{2,1,0:T(8,128)(2,1)S(1)} all-to-all(bf16[32,16,128]{2,1,0:T(8,128)(2,1)S(1)} %frame_block.3), channel_id=1, replica_groups=mesh['groups'=1,'frame'=32] {'frame'}, dimensions={0} | all-to-all | bytes 262144 | tf_op jit(solution)/shard_map/all_to_all | solution.py:373
  41.0 0.0 copy-done.4
  41.0 0.0 copy-done.6
  41.0 0.0 copy-done.8
  41.0 0.0 copy-start.10
  41.0 0.0 copy-start.12
  41.0 0.0 copy-start.14
  41.0 0.0 copy-start.15
  41.0 2.1 %track_block.3 = bf16[32,16,128]{2,1,0:T(8,128)(2,1)S(1)} custom-call(bf16[32,16,128]{2,1,0:T(8,128)(2,1)S(1)} %all_to_all.51.refs_0_, s32[32,128]{1,0:T(8,128)S(1)} %copy-done.11, f32[2,2,384]{2,1,0:T(2,128)S(1)} %copy-done.13, bf16[2,384,1152]{2,1,0:T(8,128)(2,1)S(1)} %copy-done.6, bf16[2,384,384]{2,1,0:T(8,128)(2,1)S(1)} %copy-done.8, ...), custom_call_target="tpu_custom_call" | custom-call | tf_op jit(solution)/shard_map/track_block/pallas_call | solution.py:477
  43.1 10.0 %all_to_all.52.received_ref = bf16[32,16,128]{2,1,0:T(8,128)(2,1)S(1)} all-to-all(bf16[32,16,128]{2,1,0:T(8,128)(2,1)S(1)} %track_block.3), channel_id=1, replica_groups=mesh['groups'=1,'frame'=32] {'frame'}, dimensions={0} | all-to-all | bytes 262144 | tf_op jit(solution)/shard_map/all_to_all | solution.py:373
  53.1 0.7 %layout.3 = bf16[1,128,384]{2,1,0:T(8,128)(2,1)} custom-call(bf16[32,16,128]{2,1,0:T(8,128)(2,1)S(1)} %all_to_all.52.received_ref), custom_call_target="tpu_custom_call" | custom-call | tf_op jit(solution)/shard_map/layout/pallas_call | solution.py:487
  53.8 0.0 copy-done.10
  53.8 0.0 copy-done.12
  53.8 0.0 copy-done.14
  53.8 0.0 copy-done.15
  53.8 0.8 %while.18 = (s32[]{:T(128)}, bf16[1,128,384]{2,1,0:T(8,128)(2,1)}, bf16[1,64,128,128]{3,2,1,0:T(8,128)(2,1)}, s32[1,128]{1,0:T(1,128)S(1)}, s32[1,128]{1,0:T(1,1...) while((s32[]{:T(128)}, bf16[1,128,384]{2,1,0:T(8,128)(2,1)}, ...), condition=%region_3.4_spmd, body=%region_0.3_spmd | while | flops 3 | bytes 46989864 | solution.py:506
Async XLA Ops:
  0.0 23.8 %copy-start.11 = (s32[32,128]{1,0:T(8,128)S(1)}, s32[32,128]{1,0:T(8,128)}, u32[]{:S(2)}) copy-start(s32[32,128]{1,0:T(8,128)} %refs_1_.3) | copy-start | bytes 49156
  0.0 23.8 %copy-start.13 = (f32[2,2,384]{2,1,0:T(2,128)S(1)}, f32[2,2,384]{2,1,0:T(2,128)}, u32[]{:S(2)}) copy-start(f32[2,2,384]{2,1,0:T(2,128)} %refs_2_.2) | copy-start | bytes 18436
  0.0 23.8 %copy-start.2 = (bf16[2,384,1536]{2,1,0:T(8,128)(2,1)S(1)}, bf16[2,384,1536]{2,1,0:T(8,128)(2,1)}, u32[]{:S(2)}) copy-start(bf16[2,384,1536]{2,1,0:T(8,128)(2,1)} %refs_5_.3) | copy-start | bytes 7077892
  23.8 17.2 %copy-start.4 = (bf16[2,1536,384]{2,1,0:T(8,128)(2,1)S(1)}, bf16[2,1536,384]{2,1,0:T(8,128)(2,1)}, u32[]{:S(2)}) copy-start(bf16[2,1536,384]{2,1,0:T(8,128)(2,1)} %refs_6_.5) | copy-start | bytes 7077892
  23.8 17.2 %copy-start.6 = (bf16[2,384,1152]{2,1,0:T(8,128)(2,1)S(1)}, bf16[2,384,1152]{2,1,0:T(8,128)(2,1)}, u32[]{:S(2)}) copy-start(bf16[2,384,1152]{2,1,0:T(8,128)(2,1)} %refs_3_.1) | copy-start | bytes 5308420
  23.8 17.2 %copy-start.8 = (bf16[2,384,384]{2,1,0:T(8,128)(2,1)S(1)}, bf16[2,384,384]{2,1,0:T(8,128)(2,1)}, u32[]{:S(2)}) copy-start(bf16[2,384,384]{2,1,0:T(8,128)(2,1)} %refs_4_.3) | copy-start | bytes 1769476
  41.0 12.8 %copy-start.10 = (bf16[98,384]{1,0:T(8,128)(2,1)S(1)}, bf16[98,384]{1,0:T(8,128)(2,1)}, u32[]{:S(2)}) copy-start(bf16[98,384]{1,0:T(8,128)(2,1)} %refs_6_.3) | copy-start | bytes 225796
  41.0 12.8 %copy-start.12 = (s32[128]{0:T(128)S(1)}, s32[128]{0:T(128)}, u32[]{:S(2)}) copy-start(s32[128]{0:T(128)} %param.19) | copy-start | bytes 1540
  41.0 12.8 %copy-start.14 = (s32[1,128]{1,0:T(1,128)S(1)}, s32[1,128]{1,0:T(1,128)}, u32[]{:S(2)}) copy-start(s32[1,128]{1,0:T(1,128)} %refs_4_.2) | copy-start | bytes 1540
  41.0 12.8 %copy-start.15 = (s32[1,128]{1,0:T(1,128)S(1)}, s32[1,128]{1,0:T(1,128)}, u32[]{:S(2)}) copy-start(s32[1,128]{1,0:T(1,128)} %refs_5_.2) | copy-start | bytes 1540

commit v3 on v2

--- a/solution.py
+++ b/solution.py
@@ -39,56 +39,70 @@
     return lax.dot_general(left, right, (((1,), (1,)), ((), ())), preferred_element_type=F32)
 
 
-def pack(slots, base, query, row, column, copies, cells, out_ref):
+def slot_cells(slots, base, query, row, column, breadth):
     me = lax.axis_index("frame")
     points = query.shape[1]
-    chunks, depth, breadth, channels = cells.shape
     mine = query == me
     before = jnp.where(iota((points, points), 0) < iota((points, points), 1), 1.0, 0.0).astype(BF16)
     rank = matmul(jnp.broadcast_to(jnp.where(mine, 1.0, 0.0), (8, points)).astype(BF16), before)[:1]
     slot = jnp.where(mine, rank.astype(jnp.int32) - base, -1)
-    rows = block_rows(slots)
+    rows = TILE * -(-block_rows(slots) // TILE)
     line = iota((rows, points), 0)
     held = jnp.where(line < slots, line, line - slots) == jnp.where(slot < slots, slot, -1)
 
     def gathered(values):
         return jnp.sum(jnp.where(held, values + 1, 0).astype(F32), axis=1, keepdims=True).astype(jnp.int32) - 1
 
+    is_fine = iota((rows, 1), 0) < slots
     fine_at = gathered(row * breadth + column)
     coarse_at = gathered((row >> 1) * (breadth // 2) + (column >> 1))
-    is_fine = iota((rows, 1), 0) < slots
-    wanted = jnp.where(is_fine, fine_at, coarse_at)
-    size = depth * breadth
-    place = iota((1, size), 1)
-    coarse_place = (place // breadth >> 1) * (breadth // 2) + (place % breadth >> 1)
-    both_places = jnp.where(is_fine, place, coarse_place)
-    weight = jnp.where(is_fine, 1.0, 0.25)
-    total = None
-    for chunk in range(chunks):
-        start = jnp.where(is_fine, chunk * size, chunk * size // 4)
-        chosen = jnp.where(both_places == wanted - start, weight, 0.0).astype(BF16)
-        copies[chunk].wait()
-        part = matmul(chosen, cells[chunk].reshape(size, channels))
-        total = part if total is None else total + part
-    twice = jnp.concatenate([total, total], axis=0).astype(BF16)
+    return is_fine, jnp.where(is_fine, fine_at, coarse_at)
+
+
+def slot_weights(is_fine, wanted, pair, breadth):
+    lane = iota((1, 2 * breadth), 1)
+    column = jnp.where(lane < breadth, lane, lane - breadth)
+    places = jnp.where(is_fine, lane, column >> 1)
+    start = jnp.where(is_fine, pair * (2 * breadth), pair * (breadth // 2))
+    return jnp.where(places == wanted - start, jnp.where(is_fine, 1.0, 0.25), 0.0).astype(BF16)
+
+
+def send_block(total, rows, out_ref):
+    block = total[:rows]
+    twice = jnp.concatenate([block, block], axis=0).astype(BF16)
     for pair in range(out_ref.shape[0] // (2 * rows)):
         out_ref[pair * 2 * rows : (pair + 1) * 2 * rows, :] = twice
 
 
-def map_copies(map_ref, cells, sems):
-    chunks, depth, _, _ = cells.shape
-    copies = [
-        pltpu.make_async_copy(map_ref.at[0, pl.ds(chunk * depth, depth)], cells.at[chunk], sems.at[chunk])
-        for chunk in range(chunks)
-    ]
-    for copy in copies:
-        copy.start()
-    return copies
+def map_copy(map_ref, cells, sems, chunk):
+    depth = cells.shape[1]
+    return pltpu.make_async_copy(map_ref.at[0, pl.ds(chunk * depth, depth)], cells.at[chunk], sems.at[chunk])
+
+
+def each_pair(map_ref, cells, sems, body, carry):
+    chunks, depth, breadth, channels = cells.shape
+
+    def walk(chunk, carry):
+        map_copy(map_ref, cells, sems, chunk).wait()
+        for inner in range(depth // 2):
+            both = cells[chunk, 2 * inner : 2 * inner + 2].reshape(2 * breadth, channels)
+            carry = body(chunk * (depth // 2) + inner, both, carry)
+        return carry
+
+    return lax.fori_loop(0, chunks, walk, carry)
 
 
 def pack_again_kernel(slots, round_ref, query_ref, row_ref, column_ref, map_ref, out_ref, cells, sems):
-    copies = map_copies(map_ref, cells, sems)
-    pack(slots, round_ref[0] * slots, query_ref[...], row_ref[...], column_ref[...], copies, cells, out_ref)
+    chunks, _, breadth, channels = cells.shape
+    for chunk in range(chunks):
+        map_copy(map_ref, cells, sems, chunk).start()
+    is_fine, wanted = slot_cells(slots, round_ref[0] * slots, query_ref[...], row_ref[...], column_ref[...], breadth)
+
+    def body(pair, both, total):
+        return total + matmul(slot_weights(is_fine, wanted, pair, breadth), both)
+
+    total = each_pair(map_ref, cells, sems, body, jnp.zeros((wanted.shape[0], channels), F32))
+    send_block(total, block_rows(slots), out_ref)
 
 
 def unpack_again_kernel(slots, devices, round_ref, query_ref, received_ref, before_ref, out_ref):
@@ -118,13 +132,11 @@
 
 def prepare_kernel(
     slots,
-    row_ref,
-    column_ref,
-    window_ref,
-    query_ref,
-    row_line_ref,
-    column_line_ref,
-    match_ref,
+    row_hbm,
+    column_hbm,
+    query_hbm,
+    window_hbm,
+    match_hbm,
     map_ref,
     packed_ref,
     rounds_ref,
@@ -133,64 +145,86 @@
     coarse_ref,
     spread_ref,
     embedding_ref,
+    row_ref,
+    column_ref,
+    query_ref,
+    window_ref,
+    match_ref,
+    corners_ref,
+    corner_at,
     cells,
     fine_map,
     coarse_map,
-    match,
+    map_sems,
     sems,
-    match_sem,
 ):
-    match_copy = pltpu.make_async_copy(match_ref, match, match_sem)
-    match_copy.start()
-    copies = map_copies(map_ref, cells, sems)
+    chunks, depth, breadth, channels = cells.shape
+    height = chunks * depth
+    half = breadth // 2
+    copies = [
+        pltpu.make_async_copy(source, target, sems.at[index])
+        for index, (source, target) in enumerate(
+            (
+                (row_hbm, row_ref),
+                (column_hbm, column_ref),
+                (query_hbm, query_ref),
+                (window_hbm, window_ref),
+                (match_hbm, match_ref),
+            )
+        )
+    ]
+    for copy in copies:
+        copy.start()
+    for chunk in range(chunks):
+        map_copy(map_ref, cells, map_sems, chunk).start()
     me = lax.axis_index("frame")
     points = query_ref.shape[1]
-    _, height, breadth, channels = map_ref.shape
-    depth = cells.shape[1]
-    half = breadth // 2
     rows = block_rows(slots)
     devices = packed_ref.shape[0] // rows
-    query = query_ref[...]
+    place = iota((2 * SPAN, match_ref.shape[0]), 0)
+    level, k, m = place >> 6, (place & (SPAN - 1)) >> 3, place & 7
+    at = jnp.where((k < PATCH) & (m < PATCH), (level * PATCH + k) * PATCH + m, -1)
+    pick = jnp.where(iota(place.shape, 1) == at, 1.0, 0.0).astype(BF16)
+    lane = iota((half, 2 * breadth), 1)
+    pool = jnp.where(jnp.where(lane < breadth, lane, lane - breadth) >> 1 == iota(lane.shape, 0), 0.25, 0.0)
+    pool = pool.astype(BF16)
+    coarse_map[pl.ds(height // 2 * half, 8), :] = jnp.zeros((8, channels), F32)
+    features = embedding_ref.shape[1]
+    feature = iota((1, features), 1)
+    of_sine = feature < features // 2
+    step = jnp.where(of_sine, feature, feature - features // 2).astype(F32)
+    frequency = jnp.exp(-math.log(10000.0) * step / (features // 2))
+    for copy in copies[:4]:
+        copy.wait()
+    row, column, query = row_ref[...], column_ref[...], query_ref[...]
+    corners_ref[0:1, :] = row * breadth + column - (3 * breadth + 3)
+    corners_ref[1:2, :] = (row >> 1) * half + (column >> 1) - (3 * half + 3)
+    corner_copy = pltpu.make_async_copy(corners_ref, corner_at, sems.at[5])
+    corner_copy.start()
+    is_fine, wanted = slot_cells(slots, 0, query, row, column, breadth)
     chosen_ref[...] = choose(query, devices, slots, 0)
     there = jnp.where(iota((devices, points), 0) == query, 1.0, 0.0)
     load = jnp.max(jnp.sum(there, axis=1, keepdims=True)).astype(jnp.int32)
     rounds_ref[0] = (load + slots - 1) // slots
-    place = iota((2 * SPAN, match_ref.shape[0]), 0)
-    level, k, m = place // SPAN, place % SPAN // 8, place % 8
-    wanted = jnp.where((k < PATCH) & (m < PATCH), (level * PATCH + k) * PATCH + m, -1)
-    pick = jnp.where(iota(place.shape, 1) == wanted, 1.0, 0.0).astype(BF16)
-    match_copy.wait()
-    spread_ref[...] = matmul(pick, match[...]).astype(BF16)
-    features = embedding_ref.shape[1]
-    feature = iota((1, features), 1)
-    of_sine = feature < features // 2
-    step = jnp.where(of_sine, feature, feature - features // 2).astype(F32)
-    angle = (window_ref[0] + me).astype(F32) * jnp.exp(-math.log(10000.0) * step / (features // 2))
+    copies[4].wait()
+    spread_ref[...] = matmul(pick, match_ref[...]).astype(BF16)
+    angle = (window_ref[0, 0] + me).astype(F32) * frequency
     embedding_ref[...] = jnp.where(of_sine, jnp.sin(angle), jnp.cos(angle))
-    pack(slots, 0, query, row_line_ref[...], column_line_ref[...], copies, cells, packed_ref)
-    pool = jnp.where(
-        iota((half, 2 * breadth), 1) % breadth // 2 == iota((half, 2 * breadth), 0), 0.25, 0.0
-    ).astype(BF16)
-    coarse_map[pl.ds(height // 2 * half, 8), :] = jnp.zeros((8, channels), F32)
-
-    def convert(pair, carry):
-        both = cells.reshape(height * breadth, channels)[
-            pl.ds(pl.multiple_of(pair * 2 * breadth, 2 * breadth), 2 * breadth), :
-        ]
+
+    def convert(pair, both, total):
+        product = matmul(jnp.concatenate([pool, slot_weights(is_fine, wanted, pair, breadth)], axis=0), both)
         fine_map[pl.ds(pl.multiple_of(pair * 2 * breadth, 2 * breadth), 2 * breadth), :] = both.astype(F32)
-        coarse_map[pl.ds(pl.multiple_of(pair * half, half), half), :] = matmul(pool, both).astype(BF16).astype(F32)
-        return carry
-
-    lax.fori_loop(0, height // 2, convert, 0, unroll=4)
+        coarse_map[pl.ds(pl.multiple_of(pair * half, half), half), :] = product[:half].astype(BF16).astype(F32)
+        return total + product[half:]
+
+    total = each_pair(map_ref, cells, map_sems, convert, jnp.zeros((wanted.shape[0], channels), F32))
+    send_block(total, rows, packed_ref)
     blank = jnp.zeros((8, channels), F32)
+    corner_copy.wait()
 
     def gather(point, carry):
-        row, column = row_ref[0, point], column_ref[0, point]
-        for ref, out, wide, at in (
-            (fine_map, fine_ref, breadth, row * breadth + column - (3 * breadth + 3)),
-            (coarse_map, coarse_ref, half, (row >> 1) * half + (column >> 1) - (3 * half + 3)),
-        ):
-            window = ref.at[pl.ds(at, 6 * wide + 8), :]
+        for level, (ref, wide, out) in enumerate(((fine_map, breadth, fine_ref), (coarse_map, half, coarse_ref))):
+            window = ref.at[pl.ds(corner_at[level, point], 6 * wide + 8), :]
             target = out.at[pl.ds(pl.multiple_of(point * SPAN, SPAN), SPAN), :]
             lines = [window[k * wide : k * wide + 8, :] for k in range(PATCH)] + [blank]
             for t in range(4):
@@ -200,32 +234,34 @@
     lax.fori_loop(0, points, gather, 0, unroll=8)
 
 
-def attention(queries, keyset, values, permitted):
+def attention(queries, keyset, values, bias):
     rows, features = queries.shape
     per_head = features // HEADS
     head_of = iota((1, features), 1) // per_head
-    spread = jnp.concatenate(
-        [jnp.where(head_of == head, queries, 0) for head in range(HEADS)], axis=0
-    )
-    scores = matmul_nt(spread, keyset) * (1.0 / math.sqrt(per_head))
-    outcome = None
+    spread = jnp.concatenate([jnp.where(head_of == head, queries, 0) for head in range(HEADS)], axis=0)
+    scores = matmul_nt(spread, keyset)
     parts = []
     for head in range(HEADS):
-        part = jnp.where(permitted, scores[head * rows : (head + 1) * rows], -1e30)
-        part = jnp.exp(part - jnp.max(part, axis=-1, keepdims=True))
-        parts.append((part / jnp.sum(part, axis=-1, keepdims=True)).astype(BF16))
-    mixed = matmul(jnp.concatenate(parts, axis=0), values)
-    for head in range(HEADS):
-        term = jnp.where(head_of == head, mixed[head * rows : (head + 1) * rows], 0.0)
-        outcome = term if outcome is None else outcome + term
-    return outcome.astype(BF16)
+        part = scores[head * rows : (head + 1) * rows] + bias
+        part = part - jnp.max(part, axis=-1, keepdims=True)
+        part = jnp.exp2(part * (math.log2(math.e) / math.sqrt(per_head)))
+        parts.append((part * (1.0 / jnp.sum(part, axis=-1, keepdims=True))).astype(BF16))
+    apart = jnp.concatenate([jnp.where(head_of == head, values, 0) for head in range(HEADS)], axis=0)
+    return matmul(jnp.concatenate(parts, axis=1), apart).astype(BF16)
+
+
+def gelu(value):
+    inner = math.sqrt(2.0 / math.pi)
+    lifted = value * (inner + (inner * 0.044715) * (value * value))
+    half = 0.5 * value
+    return half + half * jnp.tanh(lifted)
 
 
 def finish(stream, attended, gain, output_weight, expand_weight, reduce_weight):
-    stream = stream + matmul(attended, output_weight)
+    stream = stream + matmul(attended, output_weight())
     hidden = normalize(stream, gain).astype(BF16)
-    widened = jax.nn.gelu(matmul(hidden, expand_weight), approximate=True).astype(BF16)
-    return stream + matmul(widened, reduce_weight)
+    widened = gelu(matmul(hidden, expand_weight())).astype(BF16)
+    return stream + matmul(widened, reduce_weight())
 
 
 def frame_kernel(
@@ -238,49 +274,64 @@
     embedding_ref,
     visible_ref,
     gains_ref,
-    joint_ref,
-    output_ref,
-    expand_ref,
-    reduce_ref,
-    out_ref,
-    staged,
+    *refs,
 ):
+    sources, out_ref, staged, held, sems = refs[:4], refs[4], refs[5], refs[6:10], refs[10]
+    copies = [
+        pltpu.make_async_copy(source.at[0], target, sems.at[index])
+        for index, (source, target) in enumerate(zip(sources, held))
+    ]
+    for copy in copies:
+        copy.start()
+
+    def weight(index):
+        def ready():
+            copies[index].wait()
+            return held[index][...]
+
+        return ready
+
     me = lax.axis_index("frame")
     points = visible_ref.shape[1]
     channels = received_ref.shape[1]
     features = spread_ref.shape[1]
     devices, pad_rows, _ = out_ref.shape
-    anchors = matmul(chosen_ref[...], received_ref[...]).astype(BF16)
+    anchors = matmul(chosen_ref[...], received_ref[...])
     if extra_ref is not None:
-        anchors = anchors + extra_ref[...]
+        anchors = anchors + extra_ref[...].astype(F32)
     line, lane = iota((8, LANES), 0), iota((8, LANES), 1)
+    none = jnp.zeros((8, channels), F32)
     rows = []
-    for start in range(0, points, TILE):
-        levels = []
-        for level, ref in enumerate((fine_ref, coarse_ref)):
-            some = anchors[level * points + start : level * points + start + TILE]
-            levels.append(matmul_nt(some, ref[start * SPAN : (start + TILE) * SPAN, :]))
-        for part in range(2):
-            sides = []
-            for level, scores in enumerate(levels):
-                own = scores[part * 8 : part * 8 + 8, part * 8 * SPAN : (part + 1) * 8 * SPAN]
-                kept = own[:, :LANES]
-                for index in range(1, 4):
-                    kept = jnp.where(line // 2 == index, own[:, index * LANES : (index + 1) * LANES], kept)
-                sides.append(jnp.where(line % 2 == level, kept, pltpu.roll(kept, SPAN, 1)))
-            rows.append(jnp.where(lane < SPAN, sides[0], sides[1]))
+    for start in range(0, points, 8):
+        fine, coarse = anchors[start : start + 8], anchors[points + start : points + start + 8]
+        both = jnp.concatenate(
+            [jnp.concatenate([fine, none], axis=1), jnp.concatenate([none, coarse], axis=1)], axis=0
+        ).astype(BF16)
+        span = slice(start * SPAN, (start + 8) * SPAN)
+        scores = matmul_nt(both, jnp.concatenate([fine_ref[span, :], coarse_ref[span, :]], axis=1))
+        sides = []
+        for level in range(2):
+            own = scores[level * 8 : level * 8 + 8]
+            kept = own[:, :LANES]
+            for index in range(1, 4):
+                kept = jnp.where(line // 2 == index, own[:, index * LANES : (index + 1) * LANES], kept)
+            sides.append(jnp.where(line % 2 == level, kept, pltpu.roll(kept, SPAN, 1)))
+        rows.append(jnp.where(lane < SPAN, sides[0], sides[1]))
     matches = (jnp.concatenate(rows, axis=0) * (1.0 / math.sqrt(channels))).astype(BF16)
     tokens = (matmul(matches, spread_ref[...]) + embedding_ref[...]).astype(BF16)
 
     stream = tokens.astype(F32)
     hidden = normalize(stream, gains_ref[0, 0:1, :]).astype(BF16)
-    projected = matmul(hidden, joint_ref[0]).astype(BF16)
+    projected = matmul(hidden, weight(0)()).astype(BF16)
     allowed = visible_ref[pl.ds(me, 1), :] == 1
     permitted = allowed | (iota((points, points), 0) == iota((points, points), 1))
     attended = attention(
-        projected[:, :features], projected[:, features : 2 * features], projected[:, 2 * features :], permitted
+        projected[:, :features],
+        projected[:, features : 2 * features],
+        projected[:, 2 * features :],
+        jnp.where(permitted, 0.0, -1e30),
     )
-    crossed = finish(stream, attended, gains_ref[0, 1:2, :], output_ref[0], expand_ref[0], reduce_ref[0])
+    crossed = finish(stream, attended, gains_ref[0, 1:2, :], weight(1), weight(2), weight(3))
     chunks = features // LANES
     for i in range(points // devices):
         for c in range(chunks):
@@ -343,9 +394,16 @@
         later(projected[:, :features]),
         projected[:, features : 2 * features],
         projected[:, 2 * features :],
-        permitted,
+        jnp.where(permitted, 0.0, -1e30),
     )
-    tracked = finish(later(stream), attended, gains_ref[1, 1:2, :], output_ref[1], expand_ref[1], reduce_ref[1])
+    tracked = finish(
+        later(stream),
+        attended,
+        gains_ref[1, 1:2, :],
+        lambda: output_ref[1],
+        lambda: expand_ref[1],
+        lambda: reduce_ref[1],
+    )
     for i in range(per_device):
         for c in range(chunks):
             piece = tracked[i * rest : (i + 1) * rest, c * LANES : (c + 1) * LANES]
@@ -402,6 +460,7 @@
     map_sems = pltpu.SemaphoreType.DMA((chunks,))
     block = jax.ShapeDtypeStruct((devices * rows, channels), BF16)
 
+    line = pltpu.VMEM((1, points), jnp.int32)
     packed, rounds, *prepared = pl.pallas_call(
         lambda *refs: prepare_kernel(slots, *refs),
         out_shape=[
@@ -413,28 +472,25 @@
             jax.ShapeDtypeStruct((2 * SPAN, features), BF16),
             jax.ShapeDtypeStruct((1, features), F32),
         ],
-        in_specs=[smem, smem, smem, vmem, vmem, vmem, here, here],
+        in_specs=[here] * 6,
         out_specs=[vmem, smem] + [vmem] * 5,
         scratch_shapes=[
+            line,
+            line,
+            line,
+            pltpu.SMEM((1, 1), jnp.int32),
+            pltpu.VMEM(match_weight.shape, BF16),
+            pltpu.VMEM((2, points), jnp.int32),
+            pltpu.SMEM((2, points), jnp.int32),
             map_scratch,
             pltpu.VMEM((height * breadth, channels), F32),
             pltpu.VMEM((height * breadth // 4 + 8, channels), F32),
-            pltpu.VMEM(match_weight.shape, BF16),
             map_sems,
-            pltpu.SemaphoreType.DMA,
+            pltpu.SemaphoreType.DMA((6,)),
         ],
         compiler_params=pltpu.CompilerParams(vmem_limit_bytes=(16 + points // 16) * MIB),
         name="prepare",
-    )(
-        pixel_row,
-        pixel_column,
-        window_start,
-        query_row,
-        pixel_row,
-        pixel_column,
-        match_weight,
-        feature_map,
-    )
+    )(pixel_row, pixel_column, query_row, window_start.reshape(1, 1), match_weight, feature_map)
     rounds = rounds.reshape(())
     received = exchange(packed)
     extra = ()
@@ -467,10 +523,14 @@
     crossed = pl.pallas_call(
         frame_kernel if further else lambda *refs: frame_kernel(None, *refs),
         out_shape=jax.ShapeDtypeStruct((devices, pad_rows, LANES), BF16),
-        in_specs=[vmem] * (12 + len(extra)),
+        in_specs=[vmem] * (8 + len(extra)) + [here] * 4,
         out_specs=vmem,
-        scratch_shapes=[pltpu.VMEM((devices * pad_rows, LANES), F32)],
-        compiler_params=pltpu.CompilerParams(vmem_limit_bytes=(8 + points // 16) * MIB),
+        scratch_shapes=[
+            pltpu.VMEM((devices * pad_rows, LANES), F32),
+            *(pltpu.VMEM(array.shape[1:], BF16) for array in weights),
+            pltpu.SemaphoreType.DMA((4,)),
+        ],
+        compiler_params=pltpu.CompilerParams(vmem_limit_bytes=(12 + points // 16) * MIB),
         name="frame_block",
     )(*extra, received, *prepared, visible, layer_gains, *weights)
     by_track = exchange(crossed)

time: 55 us -> 50.9 us (0.925)
  Pallas kernels: 16.2 us -> 12.4 us
    pallas_call x1, Pallas kernels: 6.51 us -> 4.44 us  [step(): pl.pallas_call(frame_kernel if further else lambda *refs: frame_kernel(No...]
    pallas_call x1, Pallas kernels: 6.89 us -> 5.22 us  [step(): pl.pallas_call(lambda *refs: prepare_kernel(slots, *refs), out_shape=[blo...]
where the time goes in v3:
time: 50.9 us; the launch traced here: 50.7 us
  blocking collectives  36.7 us (72%)
  Pallas kernels  12.4 us (24%)
  between operations  0.9 us (2%)
  loops' own time  0.64 us (1%)
    all_to_all x3, blocking collectives, exchange(): lax.all_to_all(block, 'frame', split_axis=0, concat_axis=0, tiled=True)  36.7 us
    pallas_call x1, Pallas kernels, step(): pl.pallas_call(lambda *refs: prepare_kernel(slots, *refs), out_shape=[blo...  5.22 us
    pallas_call x1, Pallas kernels, step(): pl.pallas_call(frame_kernel if further else lambda *refs: frame_kernel(No...  4.44 us
    pallas_call x1, Pallas kernels, step(): pl.pallas_call(lambda *refs: track_kernel(per_device, *refs), out_shape=j...  2.06 us

profile of v3, /device:TPU:0, one launch (start us, length us, event | category | flops | bytes accessed | tf_op | source)
XLA Modules:
  0.0 50.7 jit_solution(2499153787168945349)
XLA Ops:
  0.0 0.0 copy-start.11
  0.0 0.0 copy-start.13
  0.0 0.0 copy-start.2
  0.8 5.2 %prepare.3 = (bf16[768,128]{1,0:T(8,128)(2,1)S(1)}, s32[1]{0:T(128)}, bf16[256,768]{1,0:T(8,128)(2,1)S(1)}, bf16[8192,128]{1,0:T(8,128)(2,1)S(1)}, bf16[8192,128...) custom-call(s32[1,128]{1,0:T(1,128)} %refs_0_.1, s32[1,128]{1,0:T(1,128)} %refs_1_.2, ...), custom_call_target="tpu_custom_call" | custom-call | tf_op jit(solution)/shard_map/prepare/pallas_call | solution.py:464
  6.0 16.1 %all_to_all.50 = bf16[32,24,128]{2,1,0:T(8,128)(2,1)S(1)} all-to-all(bf16[32,24,128]{2,1,0:T(8,128)(2,1)S(1)} %bitcast.23), channel_id=1, replica_groups=mesh['groups'=1,'frame'=32] {'frame'}, dimensions={0} | all-to-all | bytes 393216 | tf_op jit(solution)/shard_map/all_to_all | solution.py:431
  22.1 0.0 copy-done.11
  22.1 0.0 copy-done.13
  22.1 0.0 copy-done.2
  22.1 0.0 copy-start.4
  22.1 0.0 copy-start.6
  22.2 0.0 copy-start.8
  22.2 4.4 %frame_block.3 = bf16[32,16,128]{2,1,0:T(8,128)(2,1)S(1)} custom-call(bf16[768,128]{1,0:T(8,128)(2,1)S(1)} %bitcast.22, bf16[256,768]{1,0:T(8,128)(2,1)S(1)} %get-tuple-element.143.refs_1_, bf16[8192,128]{1,0:T(8,128)(2,1)S(1)} %get-tuple-element.144.refs_2_, bf16[8192,128]{1,0:T(8,128)(2,1)S(1)} %get-tuple-element.145.refs_3_, ...), custom_call_target="tpu_custom_call" | custom-call | tf_op jit(solution)/shard_map/frame_block/pallas_call | solution.py:523
  26.6 10.6 %all_to_all.51.refs_0_ = bf16[32,16,128]{2,1,0:T(8,128)(2,1)S(1)} all-to-all(bf16[32,16,128]{2,1,0:T(8,128)(2,1)S(1)} %frame_block.3), channel_id=1, replica_groups=mesh['groups'=1,'frame'=32] {'frame'}, dimensions={0} | all-to-all | bytes 262144 | tf_op jit(solution)/shard_map/all_to_all | solution.py:431
  37.2 0.0 copy-done.4
  37.2 0.0 copy-done.6
  37.2 0.0 copy-done.8
  37.2 0.0 copy-start.10
  37.3 0.0 copy-start.12
  37.3 0.0 copy-start.14
  37.3 0.0 copy-start.15
  37.3 2.1 %track_block.3 = bf16[32,16,128]{2,1,0:T(8,128)(2,1)S(1)} custom-call(bf16[32,16,128]{2,1,0:T(8,128)(2,1)S(1)} %all_to_all.51.refs_0_, s32[32,128]{1,0:T(8,128)S(1)} %copy-done.11, f32[2,2,384]{2,1,0:T(2,128)S(1)} %copy-done.13, bf16[2,384,1152]{2,1,0:T(8,128)(2,1)S(1)} %copy-done.6, bf16[2,384,384]{2,1,0:T(8,128)(2,1)S(1)} %copy-done.8, ...), custom_call_target="tpu_custom_call" | custom-call | tf_op jit(solution)/shard_map/track_block/pallas_call | solution.py:537
  39.4 10.0 %all_to_all.52.received_ref = bf16[32,16,128]{2,1,0:T(8,128)(2,1)S(1)} all-to-all(bf16[32,16,128]{2,1,0:T(8,128)(2,1)S(1)} %track_block.3), channel_id=1, replica_groups=mesh['groups'=1,'frame'=32] {'frame'}, dimensions={0} | all-to-all | bytes 262144 | tf_op jit(solution)/shard_map/all_to_all | solution.py:431
  49.3 0.7 %layout.3 = bf16[1,128,384]{2,1,0:T(8,128)(2,1)} custom-call(bf16[32,16,128]{2,1,0:T(8,128)(2,1)S(1)} %all_to_all.52.received_ref), custom_call_target="tpu_custom_call" | custom-call | tf_op jit(solution)/shard_map/layout/pallas_call | solution.py:547
  50.0 0.0 copy-done.10
  50.1 0.0 copy-done.12
  50.1 0.0 copy-done.14
  50.1 0.0 copy-done.15
  50.1 0.6 %while.18 = (s32[]{:T(128)}, bf16[1,128,384]{2,1,0:T(8,128)(2,1)}, bf16[1,64,128,128]{3,2,1,0:T(8,128)(2,1)}, s32[1,128]{1,0:T(1,128)S(1)}, s32[1,128]{1,0:T(1,1...) while((s32[]{:T(128)}, bf16[1,128,384]{2,1,0:T(8,128)(2,1)}, ...), condition=%region_3.4_spmd, body=%region_0.3_spmd | while | flops 3 | bytes 46989864 | solution.py:566
Async XLA Ops:
  0.0 22.1 %copy-start.11 = (s32[32,128]{1,0:T(8,128)S(1)}, s32[32,128]{1,0:T(8,128)}, u32[]{:S(2)}) copy-start(s32[32,128]{1,0:T(8,128)} %refs_1_.3) | copy-start | bytes 49156
  0.0 22.1 %copy-start.13 = (f32[2,2,384]{2,1,0:T(2,128)S(1)}, f32[2,2,384]{2,1,0:T(2,128)}, u32[]{:S(2)}) copy-start(f32[2,2,384]{2,1,0:T(2,128)} %refs_2_.1) | copy-start | bytes 18436
  0.0 22.1 %copy-start.2 = (bf16[2,384,1536]{2,1,0:T(8,128)(2,1)S(1)}, bf16[2,384,1536]{2,1,0:T(8,128)(2,1)}, u32[]{:S(2)}) copy-start(bf16[2,384,1536]{2,1,0:T(8,128)(2,1)} %refs_5_.3) | copy-start | bytes 7077892
  22.1 15.1 %copy-start.4 = (bf16[2,1536,384]{2,1,0:T(8,128)(2,1)S(1)}, bf16[2,1536,384]{2,1,0:T(8,128)(2,1)}, u32[]{:S(2)}) copy-start(bf16[2,1536,384]{2,1,0:T(8,128)(2,1)} %refs_6_.3) | copy-start | bytes 7077892
  22.1 15.1 %copy-start.6 = (bf16[2,384,1152]{2,1,0:T(8,128)(2,1)S(1)}, bf16[2,384,1152]{2,1,0:T(8,128)(2,1)}, u32[]{:S(2)}) copy-start(bf16[2,384,1152]{2,1,0:T(8,128)(2,1)} %refs_3_.1) | copy-start | bytes 5308420
  22.2 15.1 %copy-start.8 = (bf16[2,384,384]{2,1,0:T(8,128)(2,1)S(1)}, bf16[2,384,384]{2,1,0:T(8,128)(2,1)}, u32[]{:S(2)}) copy-start(bf16[2,384,384]{2,1,0:T(8,128)(2,1)} %refs_4_.3) | copy-start | bytes 1769476
  37.2 12.8 %copy-start.10 = (bf16[98,384]{1,0:T(8,128)(2,1)S(1)}, bf16[98,384]{1,0:T(8,128)(2,1)}, u32[]{:S(2)}) copy-start(bf16[98,384]{1,0:T(8,128)(2,1)} %refs_4_.2) | copy-start | bytes 225796
  37.3 12.8 %copy-start.12 = (s32[128]{0:T(128)S(1)}, s32[128]{0:T(128)}, u32[]{:S(2)}) copy-start(s32[128]{0:T(128)} %param.19) | copy-start | bytes 1540
  37.3 12.8 %copy-start.14 = (s32[1,128]{1,0:T(1,128)S(1)}, s32[1,128]{1,0:T(1,128)}, u32[]{:S(2)}) copy-start(s32[1,128]{1,0:T(1,128)} %refs_0_.1) | copy-start | bytes 1540
  37.3 12.8 %copy-start.15 = (s32[1,128]{1,0:T(1,128)S(1)}, s32[1,128]{1,0:T(1,128)}, u32[]{:S(2)}) copy-start(s32[1,128]{1,0:T(1,128)} %refs_1_.2) | copy-start | bytes 1540

commit v4 on v3

--- a/solution.py
+++ b/solution.py
@@ -13,6 +13,7 @@
 LANES = 128
 TILE = 16
 SPAN = 64
+SHARE = 3
 MIB = 1 << 20
 F32 = jnp.float32
 BF16 = jnp.bfloat16
@@ -39,21 +40,22 @@
     return lax.dot_general(left, right, (((1,), (1,)), ((), ())), preferred_element_type=F32)
 
 
-def slot_cells(slots, base, query, row, column, breadth):
+def slot_cells(per_device, base, query, row, column, breadth):
     me = lax.axis_index("frame")
     points = query.shape[1]
+    slots = SHARE * per_device
     mine = query == me
     before = jnp.where(iota((points, points), 0) < iota((points, points), 1), 1.0, 0.0).astype(BF16)
     rank = matmul(jnp.broadcast_to(jnp.where(mine, 1.0, 0.0), (8, points)).astype(BF16), before)[:1]
     slot = jnp.where(mine, rank.astype(jnp.int32) - base, -1)
-    rows = TILE * -(-block_rows(slots) // TILE)
-    line = iota((rows, points), 0)
-    held = jnp.where(line < slots, line, line - slots) == jnp.where(slot < slots, slot, -1)
+    rows = TILE * -(-2 * slots // TILE)
+    line = iota((rows, 1), 0)
+    is_fine = line < slots
+    held = jnp.where(is_fine, line, line - slots) == jnp.where(slot < slots, slot, -1)
 
     def gathered(values):
         return jnp.sum(jnp.where(held, values + 1, 0).astype(F32), axis=1, keepdims=True).astype(jnp.int32) - 1
 
-    is_fine = iota((rows, 1), 0) < slots
     fine_at = gathered(row * breadth + column)
     coarse_at = gathered((row >> 1) * (breadth // 2) + (column >> 1))
     return is_fine, jnp.where(is_fine, fine_at, coarse_at)
@@ -67,11 +69,12 @@
     return jnp.where(places == wanted - start, jnp.where(is_fine, 1.0, 0.25), 0.0).astype(BF16)
 
 
-def send_block(total, rows, out_ref):
-    block = total[:rows]
-    twice = jnp.concatenate([block, block], axis=0).astype(BF16)
-    for pair in range(out_ref.shape[0] // (2 * rows)):
-        out_ref[pair * 2 * rows : (pair + 1) * 2 * rows, :] = twice
+def send_block(total, out_ref):
+    per_device = out_ref.shape[1]
+    starts = [(level * SHARE + part) * per_device for part in range(SHARE) for level in range(2)]
+    pieces = [total[start : start + per_device] for start in starts]
+    block = jnp.concatenate(pieces, axis=1).astype(BF16)
+    out_ref[...] = jnp.broadcast_to(block[None], out_ref.shape)
 
 
 def map_copy(map_ref, cells, sems, chunk):
@@ -92,46 +95,48 @@
     return lax.fori_loop(0, chunks, walk, carry)
 
 
-def pack_again_kernel(slots, round_ref, query_ref, row_ref, column_ref, map_ref, out_ref, cells, sems):
+def pack_again_kernel(round_ref, query_ref, row_ref, column_ref, map_ref, out_ref, cells, sems):
     chunks, _, breadth, channels = cells.shape
+    per_device = out_ref.shape[1]
     for chunk in range(chunks):
         map_copy(map_ref, cells, sems, chunk).start()
-    is_fine, wanted = slot_cells(slots, round_ref[0] * slots, query_ref[...], row_ref[...], column_ref[...], breadth)
+    base = round_ref[0] * SHARE * per_device
+    is_fine, wanted = slot_cells(per_device, base, query_ref[...], row_ref[...], column_ref[...], breadth)
 
     def body(pair, both, total):
         return total + matmul(slot_weights(is_fine, wanted, pair, breadth), both)
 
     total = each_pair(map_ref, cells, sems, body, jnp.zeros((wanted.shape[0], channels), F32))
-    send_block(total, block_rows(slots), out_ref)
-
-
-def unpack_again_kernel(slots, devices, round_ref, query_ref, received_ref, before_ref, out_ref):
-    chosen = choose(query_ref[...], devices, slots, round_ref[0] * slots)
-    out_ref[...] = before_ref[...] + matmul(chosen, received_ref[...]).astype(BF16)
-
-
-def block_rows(slots):
-    return 8 * -(-2 * slots // 8)
-
-
-def choose(query_row, devices, slots, base):
+    send_block(total, out_ref)
+
+
+def choose(query_row, devices, per_device, base):
     points = query_row.shape[1]
     across = jnp.broadcast_to(query_row.astype(F32), (points, points))
     down = across.T
     earlier = (across == down) & (iota((points, points), 1) < iota((points, points), 0))
-    rank = jnp.sum(jnp.where(earlier, 1.0, 0.0), axis=1, keepdims=True).astype(jnp.int32)
+    rank = jnp.sum(jnp.where(earlier, 1.0, 0.0), axis=1, keepdims=True).astype(jnp.int32) - base
     frame = down[:, :1].astype(jnp.int32)
-    rows = block_rows(slots)
-    inside = (rank >= base) & (rank < base + slots)
-    fine_at = jnp.where(inside, frame * rows + rank - base, -1)
-    coarse_at = jnp.where(inside, frame * rows + slots + rank - base, -1)
-    place = iota((points, devices * rows), 1)
-    chosen = [jnp.where(place == at, 1.0, 0.0).astype(BF16) for at in (fine_at, coarse_at)]
-    return jnp.concatenate(chosen, axis=0)
+    inside = (rank >= 0) & (rank < SHARE * per_device)
+    at = (rank // per_device * devices + frame) * per_device + rank % per_device
+    place = iota((points, SHARE * devices * per_device), 1)
+    return jnp.where(place == jnp.where(inside, at, -1), 1.0, 0.0).astype(BF16)
+
+
+def take(chosen, received_ref):
+    devices, per_device, width = received_ref.shape
+    flat = received_ref[...].reshape(devices * per_device, width)
+    share = width // SHARE
+    return matmul(chosen, jnp.concatenate([flat[:, g * share : (g + 1) * share] for g in range(SHARE)], axis=0))
+
+
+def unpack_again_kernel(round_ref, query_ref, received_ref, before_ref, out_ref):
+    devices, per_device, _ = received_ref.shape
+    chosen = choose(query_ref[...], devices, per_device, round_ref[0] * SHARE * per_device)
+    out_ref[...] = before_ref[...] + take(chosen, received_ref).astype(BF16)
 
 
 def prepare_kernel(
-    slots,
     row_hbm,
     column_hbm,
     query_hbm,
@@ -179,8 +184,8 @@
         map_copy(map_ref, cells, map_sems, chunk).start()
     me = lax.axis_index("frame")
     points = query_ref.shape[1]
-    rows = block_rows(slots)
-    devices = packed_ref.shape[0] // rows
+    devices, per_device, _ = packed_ref.shape
+    slots = SHARE * per_device
     place = iota((2 * SPAN, match_ref.shape[0]), 0)
     level, k, m = place >> 6, (place & (SPAN - 1)) >> 3, place & 7
     at = jnp.where((k < PATCH) & (m < PATCH), (level * PATCH + k) * PATCH + m, -1)
@@ -201,8 +206,8 @@
     corners_ref[1:2, :] = (row >> 1) * half + (column >> 1) - (3 * half + 3)
     corner_copy = pltpu.make_async_copy(corners_ref, corner_at, sems.at[5])
     corner_copy.start()
-    is_fine, wanted = slot_cells(slots, 0, query, row, column, breadth)
-    chosen_ref[...] = choose(query, devices, slots, 0)
+    is_fine, wanted = slot_cells(per_device, 0, query, row, column, breadth)
+    chosen_ref[...] = choose(query, devices, per_device, 0)
     there = jnp.where(iota((devices, points), 0) == query, 1.0, 0.0)
     load = jnp.max(jnp.sum(there, axis=1, keepdims=True)).astype(jnp.int32)
     rounds_ref[0] = (load + slots - 1) // slots
@@ -218,7 +223,7 @@
         return total + product[half:]
 
     total = each_pair(map_ref, cells, map_sems, convert, jnp.zeros((wanted.shape[0], channels), F32))
-    send_block(total, rows, packed_ref)
+    send_block(total, packed_ref)
     blank = jnp.zeros((8, channels), F32)
     corner_copy.wait()
 
@@ -276,7 +281,7 @@
     gains_ref,
     *refs,
 ):
-    sources, out_ref, staged, held, sems = refs[:4], refs[4], refs[5], refs[6:10], refs[10]
+    sources, out_ref, held, sems = refs[:4], refs[4], refs[5:9], refs[9]
     copies = [
         pltpu.make_async_copy(source.at[0], target, sems.at[index])
         for index, (source, target) in enumerate(zip(sources, held))
@@ -293,17 +298,16 @@
 
     me = lax.axis_index("frame")
     points = visible_ref.shape[1]
-    channels = received_ref.shape[1]
+    channels = fine_ref.shape[1]
     features = spread_ref.shape[1]
-    devices, pad_rows, _ = out_ref.shape
-    anchors = matmul(chosen_ref[...], received_ref[...])
+    anchors = take(chosen_ref[...], received_ref)
     if extra_ref is not None:
         anchors = anchors + extra_ref[...].astype(F32)
     line, lane = iota((8, LANES), 0), iota((8, LANES), 1)
     none = jnp.zeros((8, channels), F32)
     rows = []
     for start in range(0, points, 8):
-        fine, coarse = anchors[start : start + 8], anchors[points + start : points + start + 8]
+        fine, coarse = anchors[start : start + 8, :channels], anchors[start : start + 8, channels:]
         both = jnp.concatenate(
             [jnp.concatenate([fine, none], axis=1), jnp.concatenate([none, coarse], axis=1)], axis=0
         ).astype(BF16)
@@ -332,99 +336,49 @@
         jnp.where(permitted, 0.0, -1e30),
     )
     crossed = finish(stream, attended, gains_ref[0, 1:2, :], weight(1), weight(2), weight(3))
-    chunks = features // LANES
-    for i in range(points // devices):
-        for c in range(chunks):
-            staged[pl.ds(i * chunks + c, devices, stride=pad_rows), :] = crossed[
-                i * devices : (i + 1) * devices, c * LANES : (c + 1) * LANES
-            ]
-    out_ref[...] = staged[...].astype(BF16).reshape(out_ref.shape)
-
-
-def track_kernel(
-    per_device,
-    received_ref,
-    visible_ref,
-    gains_ref,
-    joint_ref,
-    output_ref,
-    expand_ref,
-    reduce_ref,
-    out_ref,
-    staged,
-):
+    out_ref[...] = crossed.astype(BF16).reshape(out_ref.shape)
+
+
+def track_kernel(received_ref, visible_ref, gains_ref, joint_ref, output_ref, expand_ref, reduce_ref, out_ref):
     me = lax.axis_index("frame")
-    length, pad_rows, _ = received_ref.shape
-    features = output_ref.shape[1]
-    chunks = features // LANES
+    length, per_device, features = received_ref.shape
     points = visible_ref.shape[1]
-    devices = out_ref.shape[0]
     half_way = length // 2
-    staged[...] = received_ref[...].reshape(length * pad_rows, LANES).astype(F32)
-    stream = jnp.concatenate(
-        [
-            jnp.concatenate(
-                [staged[pl.ds(i * chunks + c, length, stride=pad_rows), :] for c in range(chunks)], axis=1
-            )
-            for i in range(per_device)
-        ],
-        axis=0,
-    )
-    total = per_device * length
+    rest = length - half_way
+    total = length * per_device
+    skipped = half_way * per_device
+    stream = received_ref[...].astype(F32).reshape(total, features)
     hidden = normalize(stream, gains_ref[1, 0:1, :]).astype(BF16)
     projected = matmul(hidden, joint_ref[1]).astype(BF16)
-
-    def later(array):
-        return jnp.concatenate(
-            [array[i * length + half_way : (i + 1) * length] for i in range(per_device)], axis=0
-        )
-
-    rest = length - half_way
-    lane = iota((points, total), 1)
-    pick = jnp.where(iota((points, total), 0) == lane // length * devices + me, 1.0, 0.0).astype(BF16)
-    seen = matmul(jnp.where(visible_ref[...] == 1, 1.0, 0.0).astype(BF16), pick)
-    seen = jnp.where(iota((length, total), 1) % length == iota((length, total), 0), seen, 0.0)
+    pick = iota((points, total), 0) == me * per_device + iota((points, total), 1) % per_device
+    seen = matmul(jnp.where(visible_ref[...] == 1, 1.0, 0.0).astype(BF16), jnp.where(pick, 1.0, 0.0).astype(BF16))
+    seen = jnp.where(iota((length, total), 1) // per_device == iota((length, total), 0), seen, 0.0)
     allowed = jnp.sum(seen, axis=0, keepdims=True) > 0.5
-    query_at = iota((per_device * rest, total), 0)
-    key_at = iota((per_device * rest, total), 1)
-    same_point = query_at // rest == key_at // length
-    same_frame = query_at % rest + half_way == key_at % length
-    permitted = same_point & (allowed | same_frame)
+    query_at = iota((rest * per_device, total), 0) + skipped
+    key_at = iota((rest * per_device, total), 1)
+    same_point = query_at % per_device == key_at % per_device
+    permitted = same_point & (allowed | (query_at == key_at))
     attended = attention(
-        later(projected[:, :features]),
+        projected[skipped:, :features],
         projected[:, features : 2 * features],
         projected[:, 2 * features :],
         jnp.where(permitted, 0.0, -1e30),
     )
     tracked = finish(
-        later(stream),
+        stream[skipped:],
         attended,
         gains_ref[1, 1:2, :],
         lambda: output_ref[1],
         lambda: expand_ref[1],
         lambda: reduce_ref[1],
     )
-    for i in range(per_device):
-        for c in range(chunks):
-            piece = tracked[i * rest : (i + 1) * rest, c * LANES : (c + 1) * LANES]
-            at = i * chunks + c
-            staged[pl.ds(at, rest, stride=pad_rows), :] = piece
-            staged[pl.ds(rest * pad_rows + at, half_way, stride=pad_rows), :] = jnp.broadcast_to(
-                piece[rest - 1 :], (half_way, LANES)
-            )
-    out_ref[...] = staged[...].astype(BF16).reshape(out_ref.shape)
-
-
-def layout_kernel(received_ref, out_ref, staged):
-    devices, pad_rows, _ = received_ref.shape
-    _, points, features = out_ref.shape
-    chunks = features // LANES
-    staged[...] = received_ref[...].reshape(devices * pad_rows, LANES).astype(F32)
-    for i in range(points // devices):
-        for c in range(chunks):
-            out_ref[0, i * devices : (i + 1) * devices, c * LANES : (c + 1) * LANES] = staged[
-                pl.ds(i * chunks + c, devices, stride=pad_rows), :
-            ].astype(BF16)
+    tracked = tracked.astype(BF16).reshape(rest, per_device, features)
+    out_ref[:rest] = tracked
+    out_ref[rest:] = jnp.broadcast_to(tracked[rest - 1 :], (half_way, per_device, features))
+
+
+def layout_kernel(received_ref, out_ref):
+    out_ref[...] = received_ref[...].astype(F32).reshape(out_ref.shape).astype(BF16)
 
 
 def exchange(block):
@@ -448,9 +402,6 @@
     features = match_weight.shape[1]
     devices = lax.axis_size("frame")
     per_device = points // devices
-    slots = 3 * per_device
-    rows = block_rows(slots)
-    pad_rows = TILE * -(-per_device * (features // LANES) // TILE)
     query_row = query_frame.reshape(1, points)
     vmem = pl.BlockSpec(memory_space=VMEM)
     smem = pl.BlockSpec(memory_space=SMEM)
@@ -458,15 +409,16 @@
     chunks = 8
     map_scratch = pltpu.VMEM((chunks, height // chunks, breadth, channels), BF16)
     map_sems = pltpu.SemaphoreType.DMA((chunks,))
-    block = jax.ShapeDtypeStruct((devices * rows, channels), BF16)
+    block = jax.ShapeDtypeStruct((devices, per_device, SHARE * 2 * channels), BF16)
+    shares = jax.ShapeDtypeStruct((devices, per_device, features), BF16)
 
     line = pltpu.VMEM((1, points), jnp.int32)
     packed, rounds, *prepared = pl.pallas_call(
-        lambda *refs: prepare_kernel(slots, *refs),
+        prepare_kernel,
         out_shape=[
             block,
             jax.ShapeDtypeStruct((1,), jnp.int32),
-            jax.ShapeDtypeStruct((2 * points, devices * rows), BF16),
+            jax.ShapeDtypeStruct((points, SHARE * devices * per_device), BF16),
             jax.ShapeDtypeStruct((points * SPAN, channels), BF16),
             jax.ShapeDtypeStruct((points * SPAN, channels), BF16),
             jax.ShapeDtypeStruct((2 * SPAN, features), BF16),
@@ -499,7 +451,7 @@
         def next_round(state):
             which, extra = state
             again = pl.pallas_call(
-                lambda *refs: pack_again_kernel(slots, *refs),
+                pack_again_kernel,
                 out_shape=block,
                 in_specs=[smem, vmem, vmem, vmem, here],
                 out_specs=vmem,
@@ -508,7 +460,7 @@
                 name="pack_again",
             )(which.reshape(1), query_row, pixel_row, pixel_column, feature_map)
             extra = pl.pallas_call(
-                lambda *refs: unpack_again_kernel(slots, devices, *refs),
+                unpack_again_kernel,
                 out_shape=jax.ShapeDtypeStruct(extra.shape, BF16),
                 in_specs=[smem, vmem, vmem, vmem],
                 out_specs=vmem,
@@ -518,15 +470,14 @@
             return which + 1, extra
 
         received, rounds = lax.optimization_barrier((received, lax.pmax(rounds, "groups")))
-        start = (jnp.int32(1), jnp.zeros((2 * points, channels), BF16))
+        start = (jnp.int32(1), jnp.zeros((points, 2 * channels), BF16))
         extra = lax.while_loop(lambda state: state[0] < rounds, next_round, start)[1:]
     crossed = pl.pallas_call(
         frame_kernel if further else lambda *refs: frame_kernel(None, *refs),
-        out_shape=jax.ShapeDtypeStruct((devices, pad_rows, LANES), BF16),
+        out_shape=shares,
         in_specs=[vmem] * (8 + len(extra)) + [here] * 4,
         out_specs=vmem,
         scratch_shapes=[
-            pltpu.VMEM((devices * pad_rows, LANES), F32),
             *(pltpu.VMEM(array.shape[1:], BF16) for array in weights),
             pltpu.SemaphoreType.DMA((4,)),
         ],
@@ -535,11 +486,10 @@
     )(*extra, received, *prepared, visible, layer_gains, *weights)
     by_track = exchange(crossed)
     tracked = pl.pallas_call(
-        lambda *refs: track_kernel(per_device, *refs),
-        out_shape=jax.ShapeDtypeStruct((devices, pad_rows, LANES), BF16),
+        track_kernel,
+        out_shape=shares,
         in_specs=[vmem] * 7,
         out_specs=vmem,
-        scratch_shapes=[pltpu.VMEM((devices * pad_rows, LANES), F32)],
         compiler_params=pltpu.CompilerParams(vmem_limit_bytes=(4 + points // 16) * MIB),
         name="track_block",
     )(by_track, visible, layer_gains, *weights)
@@ -549,7 +499,6 @@
         out_shape=jax.ShapeDtypeStruct((1, points, features), BF16),
         in_specs=[vmem],
         out_specs=vmem,
-        scratch_shapes=[pltpu.VMEM((devices * pad_rows, LANES), F32)],
         compiler_params=pltpu.CompilerParams(vmem_limit_bytes=4 * MIB),
         name="layout",
     )(arrived)

time: 50.9 us -> 49.9 us (0.980)
  blocking collectives: 36.7 us -> 35.8 us
    all_to_all x3, blocking collectives: 36.7 us -> 35.8 us  [exchange(): lax.all_to_all(block, 'frame', split_axis=0, concat_axis=0, tiled=True)]
where the time goes in v4:
time: 49.9 us; the launch traced here: 49.7 us
  blocking collectives  35.8 us (72%)
  Pallas kernels  12.2 us (24%)
  between operations  0.9 us (2%)
  loops' own time  0.7 us (1%)
    all_to_all x3, blocking collectives, exchange(): lax.all_to_all(block, 'frame', split_axis=0, concat_axis=0, tiled=True)  35.8 us
    pallas_call x1, Pallas kernels, step(): pl.pallas_call(prepare_kernel, out_shape=[block, jax.ShapeDtypeStruct((1,...  5.23 us
    pallas_call x1, Pallas kernels, step(): pl.pallas_call(frame_kernel if further else lambda *refs: frame_kernel(No...  4.33 us
    pallas_call x1, Pallas kernels, step(): pl.pallas_call(track_kernel, out_shape=shares, in_specs=[vmem] * 7, out_s...  2.02 us

profile of v4, /device:TPU:0, one launch (start us, length us, event | category | flops | bytes accessed | tf_op | source)
XLA Modules:
  0.0 49.7 jit_solution(577014136967943471)
XLA Ops:
  0.0 0.0 copy-start.10
  0.0 0.0 copy-start.12
  0.0 0.0 copy-start.2
  0.8 5.2 %prepare.3 = (bf16[32,4,768]{2,1,0:T(4,128)(2,1)S(1)}, s32[1]{0:T(128)}, bf16[128,384]{1,0:T(8,128)(2,1)S(1)}, bf16[8192,128]{1,0:T(8,128)(2,1)S(1)}, bf16[8192,...) custom-call(s32[1,128]{1,0:T(1,128)} %row_hbm.1, s32[1,128]{1,0:T(1,128)} %column_hbm.1, ...), custom_call_target="tpu_custom_call" | custom-call | tf_op jit(solution)/shard_map/prepare/pallas_call | solution.py:416
  6.0 16.1 %all_to_all.35.refs_0_ = bf16[32,4,768]{2,1,0:T(4,128)(2,1)S(1)} all-to-all(bf16[32,4,768]{2,1,0:T(4,128)(2,1)S(1)} %get-tuple-element.142), channel_id=1, replica_groups=mesh['groups'=1,'frame'=32] {'frame'}, dimensions={0} | all-to-all | bytes 393216 | tf_op jit(solution)/shard_map/all_to_all | solution.py:385
  22.1 0.0 copy-done.10
  22.1 0.0 copy-done.12
  22.1 0.0 copy-done.2
  22.1 0.0 copy-start.4
  22.2 0.0 copy-start.6
  22.2 0.0 copy-start.8
  22.2 4.3 %frame_block.3 = bf16[32,4,384]{2,1,0:T(4,128)(2,1)S(1)} custom-call(bf16[32,4,768]{2,1,0:T(4,128)(2,1)S(1)} %all_to_all.35.refs_0_, bf16[128,384]{1,0:T(8,128)(2,1)S(1)} %get-tuple-element.143.refs_1_, bf16[8192,128]{1,0:T(8,128)(2,1)S(1)} %get-tuple-element.144.refs_2_, bf16[8192,128]{1,0:T(8,128)(2,1)S(1)} %get-tuple-element.145.refs_3_, ...), custom_call_target="tpu_custom_call" | custom-call | tf_op jit(solution)/shard_map/frame_block/pallas_call | solution.py:475
  26.5 10.2 %all_to_all.36.received_ref = bf16[32,4,384]{2,1,0:T(4,128)(2,1)S(1)} all-to-all(bf16[32,4,384]{2,1,0:T(4,128)(2,1)S(1)} %frame_block.3), channel_id=1, replica_groups=mesh['groups'=1,'frame'=32] {'frame'}, dimensions={0} | all-to-all | bytes 196608 | tf_op jit(solution)/shard_map/all_to_all | solution.py:385
  36.7 0.0 copy-done.4
  36.7 0.0 copy-done.6
  36.7 0.0 copy-done.8
  36.7 0.0 copy-start.9
  36.8 0.0 copy-start.11
  36.8 0.0 copy-start.13
  36.8 0.0 copy-start.14
  36.8 2.0 %track_block.3 = bf16[32,4,384]{2,1,0:T(4,128)(2,1)S(1)} custom-call(bf16[32,4,384]{2,1,0:T(4,128)(2,1)S(1)} %all_to_all.36.received_ref, s32[32,128]{1,0:T(8,128)S(1)} %copy-done.10, f32[2,2,384]{2,1,0:T(2,128)S(1)} %copy-done.12, bf16[2,384,1152]{2,1,0:T(8,128)(2,1)S(1)} %copy-done.6, bf16[2,384,384]{2,1,0:T(8,128)(2,1)S(1)} %copy-done.8, ...), custom_call_target="tpu_custom_call" | custom-call | tf_op jit(solution)/shard_map/track_block/pallas_call | solution.py:488
  38.8 9.5 %all_to_all.37.received_ref = bf16[32,4,384]{2,1,0:T(4,128)(2,1)S(1)} all-to-all(bf16[32,4,384]{2,1,0:T(4,128)(2,1)S(1)} %track_block.3), channel_id=1, replica_groups=mesh['groups'=1,'frame'=32] {'frame'}, dimensions={0} | all-to-all | bytes 196608 | tf_op jit(solution)/shard_map/all_to_all | solution.py:385
  48.3 0.7 %layout.3 = bf16[1,128,384]{2,1,0:T(8,128)(2,1)} custom-call(bf16[32,4,384]{2,1,0:T(4,128)(2,1)S(1)} %all_to_all.37.received_ref), custom_call_target="tpu_custom_call" | custom-call | tf_op jit(solution)/shard_map/layout/pallas_call | solution.py:497
  49.0 0.0 copy-done.9
  49.0 0.0 copy-done.11
  49.0 0.0 copy-done.13
  49.0 0.0 copy-done.14
  49.0 0.7 %while.18 = (s32[]{:T(128)}, bf16[1,128,384]{2,1,0:T(8,128)(2,1)}, bf16[1,64,128,128]{3,2,1,0:T(8,128)(2,1)}, s32[1,128]{1,0:T(1,128)S(1)}, s32[1,128]{1,0:T(1,1...) while((s32[]{:T(128)}, bf16[1,128,384]{2,1,0:T(8,128)(2,1)}, ...), condition=%region_3.4_spmd, body=%region_0.3_spmd | while | flops 3 | bytes 44499468 | solution.py:515
Async XLA Ops:
  0.0 22.1 %copy-start.10 = (s32[32,128]{1,0:T(8,128)S(1)}, s32[32,128]{1,0:T(8,128)}, u32[]{:S(2)}) copy-start(s32[32,128]{1,0:T(8,128)} %visible_ref.1) | copy-start | bytes 49156
  0.0 22.1 %copy-start.12 = (f32[2,2,384]{2,1,0:T(2,128)S(1)}, f32[2,2,384]{2,1,0:T(2,128)}, u32[]{:S(2)}) copy-start(f32[2,2,384]{2,1,0:T(2,128)} %gains_ref.1) | copy-start | bytes 18436
  0.0 22.1 %copy-start.2 = (bf16[2,384,1536]{2,1,0:T(8,128)(2,1)S(1)}, bf16[2,384,1536]{2,1,0:T(8,128)(2,1)}, u32[]{:S(2)}) copy-start(bf16[2,384,1536]{2,1,0:T(8,128)(2,1)} %expand_ref.1) | copy-start | bytes 7077892
  22.1 14.6 %copy-start.4 = (bf16[2,1536,384]{2,1,0:T(8,128)(2,1)S(1)}, bf16[2,1536,384]{2,1,0:T(8,128)(2,1)}, u32[]{:S(2)}) copy-start(bf16[2,1536,384]{2,1,0:T(8,128)(2,1)} %reduce_ref.1) | copy-start | bytes 7077892
  22.2 14.6 %copy-start.6 = (bf16[2,384,1152]{2,1,0:T(8,128)(2,1)S(1)}, bf16[2,384,1152]{2,1,0:T(8,128)(2,1)}, u32[]{:S(2)}) copy-start(bf16[2,384,1152]{2,1,0:T(8,128)(2,1)} %joint_ref.1) | copy-start | bytes 5308420
  22.2 14.6 %copy-start.8 = (bf16[2,384,384]{2,1,0:T(8,128)(2,1)S(1)}, bf16[2,384,384]{2,1,0:T(8,128)(2,1)}, u32[]{:S(2)}) copy-start(bf16[2,384,384]{2,1,0:T(8,128)(2,1)} %output_ref.1) | copy-start | bytes 1769476
  36.7 12.2 %copy-start.9 = (bf16[98,384]{1,0:T(8,128)(2,1)S(1)}, bf16[98,384]{1,0:T(8,128)(2,1)}, u32[]{:S(2)}) copy-start(bf16[98,384]{1,0:T(8,128)(2,1)} %match_hbm.1) | copy-start | bytes 225796
  36.8 12.2 %copy-start.11 = (s32[128]{0:T(128)S(1)}, s32[128]{0:T(128)}, u32[]{:S(2)}) copy-start(s32[128]{0:T(128)} %param.19) | copy-start | bytes 1540
  36.8 12.2 %copy-start.13 = (s32[1,128]{1,0:T(1,128)S(1)}, s32[1,128]{1,0:T(1,128)}, u32[]{:S(2)}) copy-start(s32[1,128]{1,0:T(1,128)} %row_hbm.1) | copy-start | bytes 1540
  36.8 12.2 %copy-start.14 = (s32[1,128]{1,0:T(1,128)S(1)}, s32[1,128]{1,0:T(1,128)}, u32[]{:S(2)}) copy-start(s32[1,128]{1,0:T(1,128)} %column_hbm.1) | copy-start | bytes 1540

commit v5 on v4

--- a/solution.py
+++ b/solution.py
@@ -236,7 +236,7 @@
                 target[t * TILE : (t + 1) * TILE, :] = jnp.concatenate(lines[2 * t : 2 * t + 2], axis=0).astype(BF16)
         return carry
 
-    lax.fori_loop(0, points, gather, 0, unroll=8)
+    lax.fori_loop(0, points, gather, 0, unroll=128)
 
 
 def attention(queries, keyset, values, bias):

time: 49.9 us -> 49.4 us (0.990)
  Pallas kernels: 12.2 us -> 11.4 us
    pallas_call x1, Pallas kernels: 5.23 us -> 4.4 us  [step(): pl.pallas_call(prepare_kernel, out_shape=[block, jax.ShapeDtypeStruct((1,...]
where the time goes in v5:
time: 49.4 us; the launch traced here: 49.2 us
  blocking collectives  35.8 us (72%)
  Pallas kernels  11.4 us (23%)
  between operations  1.06 us (2%)
  loops' own time  0.88 us (2%)
    all_to_all x3, blocking collectives, exchange(): lax.all_to_all(block, 'frame', split_axis=0, concat_axis=0, tiled=True)  35.8 us
    pallas_call x1, Pallas kernels, step(): pl.pallas_call(prepare_kernel, out_shape=[block, jax.ShapeDtypeStruct((1,...  4.4 us
    pallas_call x1, Pallas kernels, step(): pl.pallas_call(frame_kernel if further else lambda *refs: frame_kernel(No...  4.35 us
    pallas_call x1, Pallas kernels, step(): pl.pallas_call(track_kernel, out_shape=shares, in_specs=[vmem] * 7, out_s...  2.02 us

profile of v5, /device:TPU:0, one launch (start us, length us, event | category | flops | bytes accessed | tf_op | source)
XLA Modules:
  0.0 49.2 jit_solution(1041976362427450958)
XLA Ops:
  0.0 0.0 copy-start.10
  0.0 0.0 copy-start.12
  0.0 0.0 copy-start.2
  0.8 4.4 %prepare.3 = (bf16[32,4,768]{2,1,0:T(4,128)(2,1)S(1)}, s32[1]{0:T(128)}, bf16[128,384]{1,0:T(8,128)(2,1)S(1)}, bf16[8192,128]{1,0:T(8,128)(2,1)S(1)}, bf16[8192,...) custom-call(s32[1,128]{1,0:T(1,128)} %row_hbm.1, s32[1,128]{1,0:T(1,128)} %column_hbm.1, ...), custom_call_target="tpu_custom_call" | custom-call | tf_op jit(solution)/shard_map/prepare/pallas_call | solution.py:416
  5.2 16.1 %all_to_all.35.refs_0_ = bf16[32,4,768]{2,1,0:T(4,128)(2,1)S(1)} all-to-all(bf16[32,4,768]{2,1,0:T(4,128)(2,1)S(1)} %get-tuple-element.142), channel_id=1, replica_groups=mesh['groups'=1,'frame'=32] {'frame'}, dimensions={0} | all-to-all | bytes 393216 | tf_op jit(solution)/shard_map/all_to_all | solution.py:385
  21.3 0.0 copy-done.10
  21.3 0.0 copy-done.12
  21.3 0.0 copy-done.2
  21.3 0.0 copy-start.4
  21.3 0.0 copy-start.6
  21.3 0.0 copy-start.8
  21.3 4.3 %frame_block.3 = bf16[32,4,384]{2,1,0:T(4,128)(2,1)S(1)} custom-call(bf16[32,4,768]{2,1,0:T(4,128)(2,1)S(1)} %all_to_all.35.refs_0_, bf16[128,384]{1,0:T(8,128)(2,1)S(1)} %get-tuple-element.143.refs_1_, bf16[8192,128]{1,0:T(8,128)(2,1)S(1)} %get-tuple-element.144.refs_2_, bf16[8192,128]{1,0:T(8,128)(2,1)S(1)} %get-tuple-element.145.refs_3_, ...), custom_call_target="tpu_custom_call" | custom-call | tf_op jit(solution)/shard_map/frame_block/pallas_call | solution.py:475
  25.7 10.2 %all_to_all.36.received_ref = bf16[32,4,384]{2,1,0:T(4,128)(2,1)S(1)} all-to-all(bf16[32,4,384]{2,1,0:T(4,128)(2,1)S(1)} %frame_block.3), channel_id=1, replica_groups=mesh['groups'=1,'frame'=32] {'frame'}, dimensions={0} | all-to-all | bytes 196608 | tf_op jit(solution)/shard_map/all_to_all | solution.py:385
  35.9 0.0 copy-done.4
  35.9 0.0 copy-done.6
  35.9 0.0 copy-done.8
  35.9 0.0 copy-start.9
  35.9 0.0 copy-start.11
  35.9 0.0 copy-start.13
  36.0 0.0 copy-start.14
  36.0 2.0 %track_block.3 = bf16[32,4,384]{2,1,0:T(4,128)(2,1)S(1)} custom-call(bf16[32,4,384]{2,1,0:T(4,128)(2,1)S(1)} %all_to_all.36.received_ref, s32[32,128]{1,0:T(8,128)S(1)} %copy-done.10, f32[2,2,384]{2,1,0:T(2,128)S(1)} %copy-done.12, bf16[2,384,1152]{2,1,0:T(8,128)(2,1)S(1)} %copy-done.6, bf16[2,384,384]{2,1,0:T(8,128)(2,1)S(1)} %copy-done.8, ...), custom_call_target="tpu_custom_call" | custom-call | tf_op jit(solution)/shard_map/track_block/pallas_call | solution.py:488
  38.0 9.5 %all_to_all.37.received_ref = bf16[32,4,384]{2,1,0:T(4,128)(2,1)S(1)} all-to-all(bf16[32,4,384]{2,1,0:T(4,128)(2,1)S(1)} %track_block.3), channel_id=1, replica_groups=mesh['groups'=1,'frame'=32] {'frame'}, dimensions={0} | all-to-all | bytes 196608 | tf_op jit(solution)/shard_map/all_to_all | solution.py:385
  47.5 0.7 %layout.3 = bf16[1,128,384]{2,1,0:T(8,128)(2,1)} custom-call(bf16[32,4,384]{2,1,0:T(4,128)(2,1)S(1)} %all_to_all.37.received_ref), custom_call_target="tpu_custom_call" | custom-call | tf_op jit(solution)/shard_map/layout/pallas_call | solution.py:497
  48.1 0.0 copy-done.9
  48.1 0.0 copy-done.11
  48.1 0.0 copy-done.13
  48.1 0.0 copy-done.14
  48.1 0.9 %while.18 = (s32[]{:T(128)}, bf16[1,128,384]{2,1,0:T(8,128)(2,1)}, bf16[1,64,128,128]{3,2,1,0:T(8,128)(2,1)}, s32[1,128]{1,0:T(1,128)S(1)}, s32[1,128]{1,0:T(1,1...) while((s32[]{:T(128)}, bf16[1,128,384]{2,1,0:T(8,128)(2,1)}, ...), condition=%region_3.4_spmd, body=%region_0.3_spmd | while | flops 3 | bytes 44499468 | solution.py:515
Async XLA Ops:
  0.0 21.3 %copy-start.10 = (s32[32,128]{1,0:T(8,128)S(1)}, s32[32,128]{1,0:T(8,128)}, u32[]{:S(2)}) copy-start(s32[32,128]{1,0:T(8,128)} %visible_ref.1) | copy-start | bytes 49156
  0.0 21.3 %copy-start.12 = (f32[2,2,384]{2,1,0:T(2,128)S(1)}, f32[2,2,384]{2,1,0:T(2,128)}, u32[]{:S(2)}) copy-start(f32[2,2,384]{2,1,0:T(2,128)} %gains_ref.1) | copy-start | bytes 18436
  0.0 21.3 %copy-start.2 = (bf16[2,384,1536]{2,1,0:T(8,128)(2,1)S(1)}, bf16[2,384,1536]{2,1,0:T(8,128)(2,1)}, u32[]{:S(2)}) copy-start(bf16[2,384,1536]{2,1,0:T(8,128)(2,1)} %expand_ref.1) | copy-start | bytes 7077892
  21.3 14.6 %copy-start.4 = (bf16[2,1536,384]{2,1,0:T(8,128)(2,1)S(1)}, bf16[2,1536,384]{2,1,0:T(8,128)(2,1)}, u32[]{:S(2)}) copy-start(bf16[2,1536,384]{2,1,0:T(8,128)(2,1)} %reduce_ref.1) | copy-start | bytes 7077892
  21.3 14.6 %copy-start.6 = (bf16[2,384,1152]{2,1,0:T(8,128)(2,1)S(1)}, bf16[2,384,1152]{2,1,0:T(8,128)(2,1)}, u32[]{:S(2)}) copy-start(bf16[2,384,1152]{2,1,0:T(8,128)(2,1)} %joint_ref.1) | copy-start | bytes 5308420
  21.3 14.6 %copy-start.8 = (bf16[2,384,384]{2,1,0:T(8,128)(2,1)S(1)}, bf16[2,384,384]{2,1,0:T(8,128)(2,1)}, u32[]{:S(2)}) copy-start(bf16[2,384,384]{2,1,0:T(8,128)(2,1)} %output_ref.1) | copy-start | bytes 1769476
  35.9 12.2 %copy-start.9 = (bf16[98,384]{1,0:T(8,128)(2,1)S(1)}, bf16[98,384]{1,0:T(8,128)(2,1)}, u32[]{:S(2)}) copy-start(bf16[98,384]{1,0:T(8,128)(2,1)} %match_hbm.1) | copy-start | bytes 225796
  35.9 12.2 %copy-start.11 = (s32[128]{0:T(128)S(1)}, s32[128]{0:T(128)}, u32[]{:S(2)}) copy-start(s32[128]{0:T(128)} %param.19) | copy-start | bytes 1540
  35.9 12.2 %copy-start.13 = (s32[1,128]{1,0:T(1,128)S(1)}, s32[1,128]{1,0:T(1,128)}, u32[]{:S(2)}) copy-start(s32[1,128]{1,0:T(1,128)} %row_hbm.1) | copy-start | bytes 1540
  36.0 12.2 %copy-start.14 = (s32[1,128]{1,0:T(1,128)S(1)}, s32[1,128]{1,0:T(1,128)}, u32[]{:S(2)}) copy-start(s32[1,128]{1,0:T(1,128)} %column_hbm.1) | copy-start | bytes 1540
